TPU v7x, 32 devices: a whole 2x2x4 slice. The times are simulated.
32 devices in a mesh: shot: 2 (over y), gx: 4 (over x, core), gy: 4 (over z).
Axes of the slice: x: 2, y: 2, z: 4, core: 2. Of those that a mesh axis runs over, the one named last changes fastest.
Arguments:
- src_p_prev: float32 [128, 64, 128], P(('shot', 'gx'), 'gy'), parts along dimension 0, may hold values from -6 to 6
- src_p_now: float32 [128, 64, 128], P(('shot', 'gx'), 'gy'), parts along dimension 0, may hold values from -6 to 6
- src_q_prev: float32 [128, 64, 128], P(('shot', 'gx'), 'gy'), parts along dimension 0, may hold values from -6 to 6
- src_q_now: float32 [128, 64, 128], P(('shot', 'gx'), 'gy'), parts along dimension 0, may hold values from -6 to 6
- rec_p_next: float32 [128, 64, 128], P(('shot', 'gx'), 'gy'), parts along dimension 0, may hold values from -6 to 6
- rec_p_now: float32 [128, 64, 128], P(('shot', 'gx'), 'gy'), parts along dimension 0, may hold values from -6 to 6
- rec_q_next: float32 [128, 64, 128], P(('shot', 'gx'), 'gy'), parts along dimension 0, may hold values from -6 to 6
- rec_q_now: float32 [128, 64, 128], P(('shot', 'gx'), 'gy'), parts along dimension 0, may hold values from -6 to 6
- velocity_term: float32 [64, 64, 128], P('gx', 'gy'), may hold values from 0.12 to 0.16
- epsilon: float32 [64, 64, 128], P('gx', 'gy'), may hold values from 0.2 to 0.4
- delta: float32 [64, 64, 128], P('gx', 'gy'), may hold values from 0 to 0.2
- tilt: float32 [64, 64, 128], P('gx', 'gy'), may hold values from 0 to 1.2
- azimuth: float32 [64, 64, 128], P('gx', 'gy'), may hold values from -3.140625 to 3.140625
- traces: float32 [32, 1024], P('shot', ('gx', 'gy')), parts along dimension 0, may hold values from -6 to 6
- receiver_x: int32 [1024], replicated, may hold values from 0 to 63
- receiver_y: int32 [1024], replicated, may hold values from 0 to 63
- segment_start: int32 [1], replicated, may hold values from 0 to 12
Outputs:
- image: float32 [128, 64, 128], P(('shot', 'gx'), 'gy'), parts along dimension 0
- rec_p_last: float32 [128, 64, 128], P(('shot', 'gx'), 'gy'), parts along dimension 0
- rec_q_last: float32 [128, 64, 128], P(('shot', 'gx'), 'gy'), parts along dimension 0
There are 2 independent parts, one for each index of `shot`. A program takes and returns all parts, laid end to end along the dimension named above; an argument that names none is the same for every part. Nothing has to cross between parts.
All inputs are finite; a program needn't handle non-finite values.
Results may differ from a plain program's by a relative error of at most 0.00021.
Values sent between devices are 32-bit elements; how exact they have to be, the bound alone decides.
A program may use at most 64 MiB of HBM per device.

v0:
```python
import jax
import jax.numpy as jnp
from jax import lax
from jax.sharding import PartitionSpec as P

STEPS = 4
REC_DEPTH = 4


def padded_2(value, sides, width):
    for axis, dim in sides:
        devices, length = (lax.axis_size(axis), value.shape[dim])
        up = [(i, (i + 1) % devices) for i in range(devices - 1)]
        down = [(j, i) for i, j in up]
        last = lax.slice_in_dim(value, length - width, length, axis=dim)
        initial = lax.slice_in_dim(value, 0, width, axis=dim)
        before = lax.ppermute(last, axis, up)
        after = lax.ppermute(initial, axis, down)
        value = jnp.concatenate([before, value, after], axis=dim)
    return value


def factors_of(velocity_term, epsilon, delta, tilt, azimuth):
    sin_tilt = jnp.sin(tilt)
    cos_tilt = jnp.cos(tilt)
    sin_azim = jnp.sin(azimuth)
    cos_azim = jnp.cos(azimuth)
    sin_square = sin_tilt * sin_tilt
    double_tilt = 2.0 * sin_tilt * cos_tilt
    return (
        velocity_term,
        1.0 + 2.0 * epsilon,
        jnp.sqrt(1.0 + 2.0 * delta),
        sin_square * cos_azim * cos_azim,
        sin_square * sin_azim * sin_azim,
        cos_tilt * cos_tilt,
        2.0 * sin_square * sin_azim * cos_azim,
        double_tilt * cos_azim,
        double_tilt * sin_azim,
    )


def rotated(padded, factors):
    center = padded[1:-1, 1:-1, 1:-1]
    d_xx = padded[2:, 1:-1, 1:-1] - 2.0 * center + padded[:-2, 1:-1, 1:-1]
    d_yy = padded[1:-1, 2:, 1:-1] - 2.0 * center + padded[1:-1, :-2, 1:-1]
    d_zz = padded[1:-1, 1:-1, 2:] - 2.0 * center + padded[1:-1, 1:-1, :-2]
    d_xy = 0.25 * (
        padded[2:, 2:, 1:-1]
        - padded[2:, :-2, 1:-1]
        - padded[:-2, 2:, 1:-1]
        + padded[:-2, :-2, 1:-1]
    )
    d_xz = 0.25 * (
        padded[2:, 1:-1, 2:]
        - padded[2:, 1:-1, :-2]
        - padded[:-2, 1:-1, 2:]
        + padded[:-2, 1:-1, :-2]
    )
    d_yz = 0.25 * (
        padded[1:-1, 2:, 2:]
        - padded[1:-1, 2:, :-2]
        - padded[1:-1, :-2, 2:]
        + padded[1:-1, :-2, :-2]
    )
    along_axis = (
        factors[3] * d_xx
        + factors[4] * d_yy
        + factors[5] * d_zz
        + factors[6] * d_xy
        + factors[7] * d_xz
        + factors[8] * d_yz
    )
    return (along_axis, d_xx + d_yy + d_zz)


def advance(wave_state, factors):
    p_prev, p_now, q_prev, q_now = wave_state
    p_axis, p_laplace = rotated(jnp.pad(p_now, 1), factors)
    q_axis = rotated(jnp.pad(q_now, 1), factors)[0]
    p_across = p_laplace - p_axis
    p_next = 2.0 * p_now - p_prev + factors[0] * (factors[1] * p_across + factors[2] * q_axis)
    q_next = 2.0 * q_now - q_prev + factors[0] * (factors[2] * p_across + q_axis)
    return (p_next, q_next)


def side_pad(array, margin):
    return jnp.pad(array, ((margin, margin), (margin, margin), (0, 0)))


def core_of(array, margin):
    return array[margin:-margin, margin:-margin]


def split_depth(stacked, count):
    return jnp.split(stacked, count, axis=2)


def exchange_rims(groups):
    nows = [member for wave_state in groups for member in (wave_state[1], wave_state[3])]
    stacked = jnp.concatenate(nows, axis=2)
    widened = split_depth(padded_2(stacked, (("gx", 0), ("gy", 1)), 1), len(nows))
    return [
        (
            side_pad(wave_state[0], 1),
            widened[2 * number],
            side_pad(wave_state[2], 1),
            widened[2 * number + 1],
        )
        for number, wave_state in enumerate(groups)
    ]


def run_round(records, factors, inside, planes, margin):
    widened = exchange_rims([record["state"] for record in records])
    for number, record in enumerate(records):
        wave_state = widened[number]
        p_next, q_next = advance(wave_state, factors)
        if record["backward"]:
            sample = STEPS - 1 - record["done"]
            p_next = p_next.at[:, :, REC_DEPTH].add(planes[sample])
        p_next = p_next * inside
        q_next = q_next * inside
        wave_state = (wave_state[1], p_next, wave_state[3], q_next)
        record["done"] = record["done"] + 1
        record["snaps"].append(core_of(p_next, margin))
        record["state"] = tuple((core_of(member, margin) for member in wave_state))


def per_device(
    src_p_prev,
    src_p_now,
    src_q_prev,
    src_q_now,
    rec_p_next,
    rec_p_now,
    rec_q_next,
    rec_q_now,
    velocity_term,
    epsilon,
    delta,
    tilt,
    azimuth,
    traces,
    receiver_x,
    receiver_y,
    segment_start,
):
    cells_x = src_p_now.shape[0]
    cells_y = src_p_now.shape[1]
    margin = 1
    earth_model = tuple(
        (side_pad(member, 1) for member in (velocity_term, epsilon, delta, tilt, azimuth))
    )
    factors = factors_of(
        earth_model[0], earth_model[1], earth_model[2], earth_model[3], earth_model[4]
    )
    x_global = (
        lax.axis_index("gx") * cells_x - margin + jnp.arange(cells_x + 2 * margin, dtype=jnp.int32)
    )
    y_global = (
        lax.axis_index("gy") * cells_y - margin + jnp.arange(cells_y + 2 * margin, dtype=jnp.int32)
    )
    inside_x = (x_global >= 0) & (x_global < cells_x * lax.axis_size("gx"))
    inside_y = (y_global >= 0) & (y_global < cells_y * lax.axis_size("gy"))
    inside = (inside_x[:, None, None] & inside_y[None, :, None]).astype(jnp.float32)
    window = lax.dynamic_slice_in_dim(traces, segment_start[0], STEPS, 0)
    everyone = lax.all_gather(window, ("gx", "gy"), axis=1, tiled=True)
    pick_x = (receiver_x[:, None] == x_global[None, :]).astype(jnp.float32)
    pick_y = (receiver_y[:, None] == y_global[None, :]).astype(jnp.float32)
    weighted = everyone[:, :, None] * pick_x[None, :, :]
    planes = jnp.einsum("krx,ry->kxy", weighted, pick_y, precision=lax.Precision.HIGHEST)
    source = {
        "state": (src_p_prev, src_p_now, src_q_prev, src_q_now),
        "backward": False,
        "done": 0,
        "snaps": [src_p_now],
    }
    receiver = {
        "state": (rec_p_next, rec_p_now, rec_q_next, rec_q_now),
        "backward": True,
        "done": 0,
        "snaps": [rec_p_now],
    }
    rounds = STEPS // margin
    for turn_index in range(rounds):
        run_round([source, receiver], factors, inside, planes, margin)
    image_sum = source["snaps"][STEPS] * receiver["snaps"][0]
    for back_index in range(1, STEPS + 1):
        image_sum = image_sum + source["snaps"][STEPS - back_index] * receiver["snaps"][back_index]
    return (image_sum, receiver["state"][1], receiver["state"][3])


def solution(mesh):
    return jax.shard_map(
        per_device,
        mesh=mesh,
        in_specs=(
            P(("shot", "gx"), "gy", None),
            P(("shot", "gx"), "gy", None),
            P(("shot", "gx"), "gy", None),
            P(("shot", "gx"), "gy", None),
            P(("shot", "gx"), "gy", None),
            P(("shot", "gx"), "gy", None),
            P(("shot", "gx"), "gy", None),
            P(("shot", "gx"), "gy", None),
            P("gx", "gy", None),
            P("gx", "gy", None),
            P("gx", "gy", None),
            P("gx", "gy", None),
            P("gx", "gy", None),
            P("shot", ("gx", "gy")),
            P(),
            P(),
            P(),
        ),
        out_specs=(
            P(("shot", "gx"), "gy", None),
            P(("shot", "gx"), "gy", None),
            P(("shot", "gx"), "gy", None),
        ),
        check_vma=False,
    )
```

profile of v0, /device:TPU:1, one launch (start us, length us, event | category | flops | bytes accessed | tf_op | source)
XLA Modules:
  0.0 141.3 jit_solution(2109060058614045298)
XLA Ops:
  3.5 4.5 %collective-permute-start = (f32[1,16,512]{2,1,0:T(8,128)S(1)}, f32[1,16,512]{2,1,0:T(8,128)S(1)}, u32[]{:S(2)}, u32[]{:S(2)}) collective-permute-start(f32[1,16,512]{2,1,0:T(8,128)S(1)} %get-tuple-element.137), channel_id=1, source_target_pairs={{0,4},{4,8},{8,12},{1,5},{5,9},{9,13},{2,6},{6,10},{10,14},{3,7},{... | collective-permute-start | bytes 98312 | tf_op jit(solution)/shard_map/ppermute | solution.py:17
  8.0 1.9 %collective-permute-start.1 = (f32[1,16,512]{2,1,0:T(8,128)S(1)}, f32[1,16,512]{2,1,0:T(8,128)S(1)}, u32[]{:S(2)}, u32[]{:S(2)}) collective-permute-start(f32[1,16,512]{2,1,0:T(8,128)S(1)} %get-tuple-element.138), channel_id=1, source_target_pairs={{4,0},{8,4},{12,8},{5,1},{9,5},{13,9},{6,2},{10,6},{14,10},{7,3},{... | collective-permute-start | bytes 98312 | tf_op jit(solution)/shard_map/ppermute | solution.py:18
  10.6 28.7 %all-gather = f32[16,64,4]{1,2,0:T(4,128)S(1)} all-gather(f32[1,64,4]{1,2,0:T(4,128)S(1)} %dynamic-slice_bitcast_fusion), channel_id=1, replica_groups=mesh['shot'=2,'gx'=4,'gy'=4] {'gx','gy'}, dimensions={0}, use_global_device_ids=true | all-gather | bytes 17408 | tf_op jit(solution)/shard_map/all_gather | solution.py:168
  43.9 3.2 %collective-permute-done.3 = f32[18,1,512]{2,1,0:T(1,128)S(1)} collective-permute-done((f32[18,1,512]{2,1,0:T(1,128)S(1)}, f32[18,1,512]{2,1,0:T(1,128)S(1)}, u32[]{:S(2)}, u32[]{:S(2)}) %collective-permute-start.3) | collective-permute-done | bytes 36896 | tf_op jit(solution)/shard_map/ppermute | solution.py:18
  48.5 3.0 %broadcast_multiply_fusion.10 = (f32[18,18,128]{2,1,0:T(8,128)S(1)}, f32[18,18,128]{2,1,0:T(8,128)S(1)}, f32[18,18,128]{2,1,0:T(8,128)S(1)}, f32[18,18,128]{2,1,...) fusion(f32[18,18,512]{2,1,0:T(8,128)S(1)} %pad_maximum_fusion, ...), kind=kLoop, calls=%fused_computation.842 | loop fusion | flops 3732480 | bytes 3440640 | tf_op jit(solution)/shard_map/mul | solution.py:82
  53.2 2.8 %fusion.31 = (f32[18,18,128]{2,1,0:T(8,128)S(1)}, f32[18,18,128]{2,1,0:T(8,128)S(1)}) fusion(f32[16,16,128]{2,1,0:T(8,128)S(1)} %copy-done.3, f32[18,18,128]{2,1,0:T(8,128)S(1)} %get-tuple-element.114, f32[16,16,128]{2,1,0:T(8,128)S(1)} %copy-done.2, f32[18,18,128]{2,1,0:T(8,128)S(1)} %get-tuple-element.113), kind=kLoop, calls=%fused_computation.333 | loop fusion | flops 3151872 | bytes 925696 | tf_op jit(solution)/shard_map/sub | solution.py:81
  57.2 7.8 %collective-permute-start.4 = (f32[1,16,512]{2,1,0:T(8,128)S(1)}, f32[1,16,512]{2,1,0:T(8,128)S(1)}, u32[]{:S(2)}, u32[]{:S(2)}) collective-permute-start(f32[1,16,512]{2,1,0:T(8,128)S(1)} %get-tuple-element.135), channel_id=1, source_target_pairs={{0,4},{4,8},{8,12},{1,5},{5,9},{9,13},{2,6},{6,10},{10,14},{3,7},{... | collective-permute-start | bytes 98312 | tf_op jit(solution)/shard_map/ppermute | solution.py:17
  65.0 1.9 %collective-permute-start.5 = (f32[1,16,512]{2,1,0:T(8,128)S(1)}, f32[1,16,512]{2,1,0:T(8,128)S(1)}, u32[]{:S(2)}, u32[]{:S(2)}) collective-permute-start(f32[1,16,512]{2,1,0:T(8,128)S(1)} %get-tuple-element.136), channel_id=1, source_target_pairs={{4,0},{8,4},{12,8},{5,1},{9,5},{13,9},{6,2},{10,6},{14,10},{7,3},{... | collective-permute-start | bytes 98312 | tf_op jit(solution)/shard_map/ppermute | solution.py:18
  66.9 3.3 %collective-permute-done.5 = f32[1,16,512]{2,1,0:T(8,128)S(1)} collective-permute-done((f32[1,16,512]{2,1,0:T(8,128)S(1)}, f32[1,16,512]{2,1,0:T(8,128)S(1)}, u32[]{:S(2)}, u32[]{:S(2)}) %collective-permute-start.5) | collective-permute-done | bytes 32800 | tf_op jit(solution)/shard_map/ppermute | solution.py:18
  70.3 2.4 %collective-permute-start.6 = (f32[18,1,512]{2,1,0:T(1,128)S(1)}, f32[18,1,512]{2,1,0:T(1,128)S(1)}, u32[]{:S(2)}, u32[]{:S(2)}) collective-permute-start(f32[18,1,512]{2,1,0:T(1,128)S(1)} %get-tuple-element.127), channel_id=1, source_target_pairs={{0,1},{1,2},{2,3},{4,5},{5,6},{6,7},{8,9},{9,10},{10,11},{12,13},{... | collective-permute-start | bytes 110600 | tf_op jit(solution)/shard_map/ppermute | solution.py:17
  74.0 3.4 %collective-permute-done.7 = f32[18,1,512]{2,1,0:T(1,128)S(1)} collective-permute-done((f32[18,1,512]{2,1,0:T(1,128)S(1)}, f32[18,1,512]{2,1,0:T(1,128)S(1)}, u32[]{:S(2)}, u32[]{:S(2)}) %collective-permute-start.7) | collective-permute-done | bytes 36896 | tf_op jit(solution)/shard_map/ppermute | solution.py:18
  77.6 3.8 %broadcast_multiply_fusion.6 = (f32[18,18,128]{2,1,0:T(8,128)}, f32[18,18,128]{2,1,0:T(8,128)}, f32[18,18,128]{2,1,0:T(8,128)S(1)}, f32[18,18,128]{2,1,0:T(8,128...) fusion(f32[18,18,512]{2,1,0:T(8,128)S(1)} %pad_maximum_fusion.1, ...), kind=kLoop, calls=%fused_computation.838 | loop fusion | flops 3732480 | bytes 3108864 | tf_op jit(solution)/shard_map/mul | solution.py:45
  83.0 2.8 %fusion.49 = (f32[18,18,128]{2,1,0:T(8,128)S(1)}, f32[18,18,128]{2,1,0:T(8,128)S(1)}) fusion(f32[16,16,128]{2,1,0:T(8,128)S(1)} %copy-done.3, f32[18,18,128]{2,1,0:T(8,128)S(1)} %get-tuple-element.104, f32[16,16,128]{2,1,0:T(8,128)S(1)} %copy-done.2, f32[18,18,128]{2,1,0:T(8,128)S(1)} %get-tuple-element.103), kind=kLoop, calls=%fused_computation.351 | loop fusion | flops 3151872 | bytes 925696 | tf_op jit(solution)/shard_map/sub | solution.py:81
  87.2 3.3 %collective-permute-start.8 = (f32[1,16,512]{2,1,0:T(8,128)S(1)}, f32[1,16,512]{2,1,0:T(8,128)S(1)}, u32[]{:S(2)}, u32[]{:S(2)}) collective-permute-start(f32[1,16,512]{2,1,0:T(8,128)S(1)} %get-tuple-element.133), channel_id=1, source_target_pairs={{0,4},{4,8},{8,12},{1,5},{5,9},{9,13},{2,6},{6,10},{10,14},{3,7},{... | collective-permute-start | bytes 98312 | tf_op jit(solution)/shard_map/ppermute | solution.py:17
  90.6 1.9 %collective-permute-start.9 = (f32[1,16,512]{2,1,0:T(8,128)S(1)}, f32[1,16,512]{2,1,0:T(8,128)S(1)}, u32[]{:S(2)}, u32[]{:S(2)}) collective-permute-start(f32[1,16,512]{2,1,0:T(8,128)S(1)} %get-tuple-element.134), channel_id=1, source_target_pairs={{4,0},{8,4},{12,8},{5,1},{9,5},{13,9},{6,2},{10,6},{14,10},{7,3},{... | collective-permute-start | bytes 98312 | tf_op jit(solution)/shard_map/ppermute | solution.py:18
  92.5 3.3 %collective-permute-done.9 = f32[1,16,512]{2,1,0:T(8,128)S(1)} collective-permute-done((f32[1,16,512]{2,1,0:T(8,128)S(1)}, f32[1,16,512]{2,1,0:T(8,128)S(1)}, u32[]{:S(2)}, u32[]{:S(2)}) %collective-permute-start.9) | collective-permute-done | bytes 32800 | tf_op jit(solution)/shard_map/ppermute | solution.py:18
  98.8 3.4 %collective-permute-done.11 = f32[18,1,512]{2,1,0:T(1,128)S(1)} collective-permute-done((f32[18,1,512]{2,1,0:T(1,128)S(1)}, f32[18,1,512]{2,1,0:T(1,128)S(1)}, u32[]{:S(2)}, u32[]{:S(2)}) %collective-permute-start.11) | collective-permute-done | bytes 36896 | tf_op jit(solution)/shard_map/ppermute | solution.py:18
  102.4 3.8 %broadcast_multiply_fusion.4 = (f32[18,18,128]{2,1,0:T(8,128)}, f32[18,18,128]{2,1,0:T(8,128)}, f32[18,18,128]{2,1,0:T(8,128)S(1)}, f32[18,18,128]{2,1,0:T(8,128...) fusion(f32[18,18,512]{2,1,0:T(8,128)S(1)} %pad_maximum_fusion.2, ...), kind=kLoop, calls=%fused_computation.836 | loop fusion | flops 3732480 | bytes 3108864 | tf_op jit(solution)/shard_map/mul | solution.py:82
  107.9 6.6 %fusion.67 = (f32[18,18,128]{2,1,0:T(8,128)S(1)}, f32[18,18,128]{2,1,0:T(8,128)S(1)}) fusion(f32[16,16,128]{2,1,0:T(8,128)S(1)} %copy-done.3, f32[18,18,128]{2,1,0:T(8,128)} %get-tuple-element.94, f32[16,16,128]{2,1,0:T(8,128)S(1)} %copy-done.2, f32[18,18,128]{2,1,0:T(8,128)S(1)} %get-tuple-element.93), kind=kLoop, calls=%fused_computation.369 | loop fusion | flops 3151872 | bytes 925696 | tf_op jit(solution)/shard_map/sub | solution.py:81
  115.7 3.3 %collective-permute-start.12 = (f32[1,16,512]{2,1,0:T(8,128)S(1)}, f32[1,16,512]{2,1,0:T(8,128)S(1)}, u32[]{:S(2)}, u32[]{:S(2)}) collective-permute-start(f32[1,16,512]{2,1,0:T(8,128)S(1)} %get-tuple-element.131), channel_id=1, source_target_pairs={{0,4},{4,8},{8,12},{1,5},{5,9},{9,13},{2,6},{6,10},{10,14},{3,7},{... | collective-permute-start | bytes 98312 | tf_op jit(solution)/shard_map/ppermute | solution.py:17
  121.0 3.3 %collective-permute-done.13 = f32[1,16,512]{2,1,0:T(8,128)S(1)} collective-permute-done((f32[1,16,512]{2,1,0:T(8,128)S(1)}, f32[1,16,512]{2,1,0:T(8,128)S(1)}, u32[]{:S(2)}, u32[]{:S(2)}) %collective-permute-start.13) | collective-permute-done | bytes 32800 | tf_op jit(solution)/shard_map/ppermute | solution.py:18
  127.5 3.2 %collective-permute-done.15 = f32[18,1,512]{2,1,0:T(1,128)S(1)} collective-permute-done((f32[18,1,512]{2,1,0:T(1,128)S(1)}, f32[18,1,512]{2,1,0:T(1,128)S(1)}, u32[]{:S(2)}, u32[]{:S(2)}) %collective-permute-start.15) | collective-permute-done | bytes 36896 | tf_op jit(solution)/shard_map/ppermute | solution.py:18
  130.9 4.3 %broadcast_multiply_fusion = (f32[18,18,128]{2,1,0:T(8,128)}, f32[18,18,128]{2,1,0:T(8,128)}, f32[18,18,128]{2,1,0:T(8,128)}, f32[18,18,128]{2,1,0:T(8,128)}, f3...) fusion(f32[18,18,512]{2,1,0:T(8,128)S(1)} %pad_maximum_fusion.3, ...), kind=kLoop, calls=%fused_computation.832 | loop fusion | flops 5225472 | bytes 2942976 | tf_op jit(solution)/shard_map/mul | solution.py:45
  136.9 2.3 %fusion.87 = (f32[18,18,128]{2,1,0:T(8,128)S(1)}, f32[18,18,128]{2,1,0:T(8,128)S(1)}) fusion(f32[16,16,128]{2,1,0:T(8,128)S(1)} %copy-done.3, f32[18,18,128]{2,1,0:T(8,128)S(1)} %get-tuple-element.85, f32[16,16,128]{2,1,0:T(8,128)S(1)} %copy-done.2), kind=kLoop, calls=%fused_computation.389 | loop fusion | flops 1741824 | bytes 759808 | tf_op jit(solution)/shard_map/add | solution.py:67
  (130 shorter events, 31.0 us)
Async XLA Ops:
  0.6 10.0 %copy-start = (f32[16,64]{1,0:T(8,128)S(1)}, f32[16,64]{1,0:T(8,128)}, u32[]{:S(2)}) copy-start(f32[16,64]{1,0:T(8,128)} %param.38) | copy-start | bytes 12292
  3.5 37.6 %collective-permute-start = (f32[1,16,512]{2,1,0:T(8,128)S(1)}, f32[1,16,512]{2,1,0:T(8,128)S(1)}, u32[]{:S(2)}, u32[]{:S(2)}) collective-permute-start(f32[1,16,512]{2,1,0:T(8,128)S(1)} %get-tuple-element.137), channel_id=1, source_target_pairs={{0,4},{4,8},{8,12},{1,5},{5,9},{9,13},{2,6},{6,10},{10,14},{3,7},{... | collective-permute-start | bytes 98312 | tf_op jit(solution)/shard_map/ppermute | solution.py:17
  8.0 33.1 %collective-permute-start.1 = (f32[1,16,512]{2,1,0:T(8,128)S(1)}, f32[1,16,512]{2,1,0:T(8,128)S(1)}, u32[]{:S(2)}, u32[]{:S(2)}) collective-permute-start(f32[1,16,512]{2,1,0:T(8,128)S(1)} %get-tuple-element.138), channel_id=1, source_target_pairs={{4,0},{8,4},{12,8},{5,1},{9,5},{13,9},{6,2},{10,6},{14,10},{7,3},{... | collective-permute-start | bytes 98312 | tf_op jit(solution)/shard_map/ppermute | solution.py:18
  41.2 2.8 %collective-permute-start.2 = (f32[18,1,512]{2,1,0:T(1,128)S(1)}, f32[18,1,512]{2,1,0:T(1,128)S(1)}, u32[]{:S(2)}, u32[]{:S(2)}) collective-permute-start(f32[18,1,512]{2,1,0:T(1,128)S(1)} %get-tuple-element.129), channel_id=1, source_target_pairs={{0,1},{1,2},{2,3},{4,5},{5,6},{6,7},{8,9},{9,10},{10,11},{12,13},{... | collective-permute-start | bytes 110600 | tf_op jit(solution)/shard_map/ppermute | solution.py:17
  42.5 4.7 %collective-permute-start.3 = (f32[18,1,512]{2,1,0:T(1,128)S(1)}, f32[18,1,512]{2,1,0:T(1,128)S(1)}, u32[]{:S(2)}, u32[]{:S(2)}) collective-permute-start(f32[18,1,512]{2,1,0:T(1,128)S(1)} %get-tuple-element.130), channel_id=1, source_target_pairs={{1,0},{2,1},{3,2},{5,4},{6,5},{7,6},{9,8},{10,9},{11,10},{13,12},{... | collective-permute-start | bytes 110600 | tf_op jit(solution)/shard_map/ppermute | solution.py:18
  53.2 2.8 %copy-start.28 = (f32[16,16,128]{2,1,0:T(8,128)S(1)}, f32[16,16,128]{2,1,0:T(8,128)}, u32[]{:S(2)}) copy-start(f32[16,16,128]{2,1,0:T(8,128)} %param.31) | copy-start | bytes 393220
  57.2 9.8 %collective-permute-start.4 = (f32[1,16,512]{2,1,0:T(8,128)S(1)}, f32[1,16,512]{2,1,0:T(8,128)S(1)}, u32[]{:S(2)}, u32[]{:S(2)}) collective-permute-start(f32[1,16,512]{2,1,0:T(8,128)S(1)} %get-tuple-element.135), channel_id=1, source_target_pairs={{0,4},{4,8},{8,12},{1,5},{5,9},{9,13},{2,6},{6,10},{10,14},{3,7},{... | collective-permute-start | bytes 98312 | tf_op jit(solution)/shard_map/ppermute | solution.py:17
  65.0 5.2 %collective-permute-start.5 = (f32[1,16,512]{2,1,0:T(8,128)S(1)}, f32[1,16,512]{2,1,0:T(8,128)S(1)}, u32[]{:S(2)}, u32[]{:S(2)}) collective-permute-start(f32[1,16,512]{2,1,0:T(8,128)S(1)} %get-tuple-element.136), channel_id=1, source_target_pairs={{4,0},{8,4},{12,8},{5,1},{9,5},{13,9},{6,2},{10,6},{14,10},{7,3},{... | collective-permute-start | bytes 98312 | tf_op jit(solution)/shard_map/ppermute | solution.py:18
  70.3 3.7 %collective-permute-start.6 = (f32[18,1,512]{2,1,0:T(1,128)S(1)}, f32[18,1,512]{2,1,0:T(1,128)S(1)}, u32[]{:S(2)}, u32[]{:S(2)}) collective-permute-start(f32[18,1,512]{2,1,0:T(1,128)S(1)} %get-tuple-element.127), channel_id=1, source_target_pairs={{0,1},{1,2},{2,3},{4,5},{5,6},{6,7},{8,9},{9,10},{10,11},{12,13},{... | collective-permute-start | bytes 110600 | tf_op jit(solution)/shard_map/ppermute | solution.py:17
  72.7 4.7 %collective-permute-start.7 = (f32[18,1,512]{2,1,0:T(1,128)S(1)}, f32[18,1,512]{2,1,0:T(1,128)S(1)}, u32[]{:S(2)}, u32[]{:S(2)}) collective-permute-start(f32[18,1,512]{2,1,0:T(1,128)S(1)} %get-tuple-element.128), channel_id=1, source_target_pairs={{1,0},{2,1},{3,2},{5,4},{6,5},{7,6},{9,8},{10,9},{11,10},{13,12},{... | collective-permute-start | bytes 110600 | tf_op jit(solution)/shard_map/ppermute | solution.py:18
  83.0 2.8 %copy-start.17 = (f32[18,18,128]{2,1,0:T(8,128)S(1)}, f32[18,18,128]{2,1,0:T(8,128)}, u32[]{:S(2)}) copy-start(f32[18,18,128]{2,1,0:T(8,128)} %get-tuple-element.100) | copy-start | bytes 497668
  83.0 2.8 %copy-start.18 = (f32[18,18,128]{2,1,0:T(8,128)S(1)}, f32[18,18,128]{2,1,0:T(8,128)}, u32[]{:S(2)}) copy-start(f32[18,18,128]{2,1,0:T(8,128)} %get-tuple-element.101) | copy-start | bytes 497668
  83.0 2.8 %copy-start.19 = (f32[18,18,128]{2,1,0:T(8,128)S(1)}, f32[18,18,128]{2,1,0:T(8,128)}, u32[]{:S(2)}) copy-start(f32[18,18,128]{2,1,0:T(8,128)} %get-tuple-element.102) | copy-start | bytes 497668
  87.2 5.3 %collective-permute-start.8 = (f32[1,16,512]{2,1,0:T(8,128)S(1)}, f32[1,16,512]{2,1,0:T(8,128)S(1)}, u32[]{:S(2)}, u32[]{:S(2)}) collective-permute-start(f32[1,16,512]{2,1,0:T(8,128)S(1)} %get-tuple-element.133), channel_id=1, source_target_pairs={{0,4},{4,8},{8,12},{1,5},{5,9},{9,13},{2,6},{6,10},{10,14},{3,7},{... | collective-permute-start | bytes 98312 | tf_op jit(solution)/shard_map/ppermute | solution.py:17
  90.6 5.2 %collective-permute-start.9 = (f32[1,16,512]{2,1,0:T(8,128)S(1)}, f32[1,16,512]{2,1,0:T(8,128)S(1)}, u32[]{:S(2)}, u32[]{:S(2)}) collective-permute-start(f32[1,16,512]{2,1,0:T(8,128)S(1)} %get-tuple-element.134), channel_id=1, source_target_pairs={{4,0},{8,4},{12,8},{5,1},{9,5},{13,9},{6,2},{10,6},{14,10},{7,3},{... | collective-permute-start | bytes 98312 | tf_op jit(solution)/shard_map/ppermute | solution.py:18
  95.9 3.0 %collective-permute-start.10 = (f32[18,1,512]{2,1,0:T(1,128)S(1)}, f32[18,1,512]{2,1,0:T(1,128)S(1)}, u32[]{:S(2)}, u32[]{:S(2)}) collective-permute-start(f32[18,1,512]{2,1,0:T(1,128)S(1)} %get-tuple-element.125), channel_id=1, source_target_pairs={{0,1},{1,2},{2,3},{4,5},{5,6},{6,7},{8,9},{9,10},{10,11},{12,13},{... | collective-permute-start | bytes 110600 | tf_op jit(solution)/shard_map/ppermute | solution.py:17
  97.5 4.7 %collective-permute-start.11 = (f32[18,1,512]{2,1,0:T(1,128)S(1)}, f32[18,1,512]{2,1,0:T(1,128)S(1)}, u32[]{:S(2)}, u32[]{:S(2)}) collective-permute-start(f32[18,1,512]{2,1,0:T(1,128)S(1)} %get-tuple-element.126), channel_id=1, source_target_pairs={{1,0},{2,1},{3,2},{5,4},{6,5},{7,6},{9,8},{10,9},{11,10},{13,12},{... | collective-permute-start | bytes 110600 | tf_op jit(solution)/shard_map/ppermute | solution.py:18
  107.9 6.6 %copy-start.14 = (f32[18,18,128]{2,1,0:T(8,128)S(1)}, f32[18,18,128]{2,1,0:T(8,128)}, u32[]{:S(2)}) copy-start(f32[18,18,128]{2,1,0:T(8,128)} %get-tuple-element.90) | copy-start | bytes 497668
  107.9 6.6 %copy-start.15 = (f32[18,18,128]{2,1,0:T(8,128)S(1)}, f32[18,18,128]{2,1,0:T(8,128)}, u32[]{:S(2)}) copy-start(f32[18,18,128]{2,1,0:T(8,128)} %get-tuple-element.91) | copy-start | bytes 497668
  107.9 6.6 %copy-start.16 = (f32[18,18,128]{2,1,0:T(8,128)S(1)}, f32[18,18,128]{2,1,0:T(8,128)}, u32[]{:S(2)}) copy-start(f32[18,18,128]{2,1,0:T(8,128)} %get-tuple-element.92) | copy-start | bytes 497668
  115.7 5.3 %collective-permute-start.12 = (f32[1,16,512]{2,1,0:T(8,128)S(1)}, f32[1,16,512]{2,1,0:T(8,128)S(1)}, u32[]{:S(2)}, u32[]{:S(2)}) collective-permute-start(f32[1,16,512]{2,1,0:T(8,128)S(1)} %get-tuple-element.131), channel_id=1, source_target_pairs={{0,4},{4,8},{8,12},{1,5},{5,9},{9,13},{2,6},{6,10},{10,14},{3,7},{... | collective-permute-start | bytes 98312 | tf_op jit(solution)/shard_map/ppermute | solution.py:17
  119.1 5.2 %collective-permute-start.13 = (f32[1,16,512]{2,1,0:T(8,128)S(1)}, f32[1,16,512]{2,1,0:T(8,128)S(1)}, u32[]{:S(2)}, u32[]{:S(2)}) collective-permute-start(f32[1,16,512]{2,1,0:T(8,128)S(1)} %get-tuple-element.132), channel_id=1, source_target_pairs={{4,0},{8,4},{12,8},{5,1},{9,5},{13,9},{6,2},{10,6},{14,10},{7,3},{... | collective-permute-start | bytes 98312 | tf_op jit(solution)/shard_map/ppermute | solution.py:18
  124.4 3.1 %collective-permute-start.14 = (f32[18,1,512]{2,1,0:T(1,128)S(1)}, f32[18,1,512]{2,1,0:T(1,128)S(1)}, u32[]{:S(2)}, u32[]{:S(2)}) collective-permute-start(f32[18,1,512]{2,1,0:T(1,128)S(1)} %get-tuple-element.123), channel_id=1, source_target_pairs={{0,1},{1,2},{2,3},{4,5},{5,6},{6,7},{8,9},{9,10},{10,11},{12,13},{... | collective-permute-start | bytes 110600 | tf_op jit(solution)/shard_map/ppermute | solution.py:17
  126.0 4.7 %collective-permute-start.15 = (f32[18,1,512]{2,1,0:T(1,128)S(1)}, f32[18,1,512]{2,1,0:T(1,128)S(1)}, u32[]{:S(2)}, u32[]{:S(2)}) collective-permute-start(f32[18,1,512]{2,1,0:T(1,128)S(1)} %get-tuple-element.124), channel_id=1, source_target_pairs={{1,0},{2,1},{3,2},{5,4},{6,5},{7,6},{9,8},{10,9},{11,10},{13,12},{... | collective-permute-start | bytes 110600 | tf_op jit(solution)/shard_map/ppermute | solution.py:18
  (25 other events, 28.5 us)
where the time goes:
time: 142 us; the launch traced here: 141 us
  starting transfers between devices  39 us (27%)
  other arithmetic  33.5 us (24%)
  blocking collectives  28.7 us (20%)
  waiting for transfers between devices  23.2 us (16%)
  local copies, waits for them, and re-layouts  14.5 us (10%)
  between operations  2.13 us (2%)
    all_gather x1, blocking collectives, per_device(): everyone = lax.all_gather(window, ('gx', 'gy'), axis=1, tiled=True)  28.7 us
    ppermute x8, starting transfers between devices, padded_2(): before = lax.ppermute(last, axis, up)  26 us
    ppermute x8, waiting for transfers between devices, padded_2(): after = lax.ppermute(initial, axis, down)  23.1 us
    ppermute x8, starting transfers between devices, padded_2(): after = lax.ppermute(initial, axis, down)  13 us
    sub x3, other arithmetic, advance(): p_across = p_laplace - p_axis  12.1 us
    unnamed x71, local copies, waits for them, and re-layouts  8.43 us
    mul x2, other arithmetic, rotated(): d_xx = padded[2:, 1:-1, 1:-1] - 2.0 * center + padded[:-2, 1:-1, 1:-1]  8.05 us
    mul x2, other arithmetic, advance(): 2.0 * p_now - p_prev  6.82 us
  transfers between devices with their start and end apart: 16, of which 7 were waited for; matrix products, arithmetic and copies ran while one was open for 1% of the time, Pallas kernels for 0%

commit v1 on v0

v1 whole, which is shorter than its diff:
```python
import functools

import jax
import jax.numpy as jnp
from jax import lax
from jax.experimental import pallas as pl
from jax.experimental.pallas import tpu as pltpu
from jax.sharding import PartitionSpec as P

STEPS = 4
REC_DEPTH = 4
TOP = 8
LANES = 128
DIRS = tuple((dx, dy) for dx in (-1, 0, 1) for dy in (-1, 0, 1) if (dx, dy) != (0, 0))
DIRS = tuple(sorted(DIRS, key=lambda d: abs(d[0]) + abs(d[1])))
MESH = pl.DeviceIdType.MESH


def sine(x):
    s = x * x
    c = 1.6059044e-10
    for k in (-2.5052108e-8, 2.7557319e-6, -1.98412698e-4, 8.3333333e-3, -1.66666667e-1):
        c = c * s + k
    return x + x * (s * c)


def cosine(x):
    s = x * x
    c = -1.1470746e-11
    for k in (2.0876757e-9, -2.7557319e-7, 2.4801587e-5, -1.38888889e-3, 4.16666667e-2, -0.5):
        c = c * s + k
    return 1.0 + s * c


def kernel(sizes, *refs):
    n_gx, n_gy, nx, ny, nz, local_rec, n_rec = sizes
    fields, model = refs[:8], refs[8:13]
    traces, rec_x, rec_y, start = refs[13:17]
    image, p_last, q_last = refs[17:20]
    (waves, olds, coef, earth, inject, rows, window, gathered, rec_pos,
     load_sem, send_sem, recv_sem, far_send, far_recv) = refs[20:]
    n = n_gx * n_gy
    gx, gy = lax.axis_index("gx"), lax.axis_index("gy")
    me = gx * n_gy + gy

    barrier = pltpu.get_barrier_semaphore()

    def peer_id(i):
        peer = lax.rem(me + i, n)
        return {"gx": peer // n_gy, "gy": lax.rem(peer, n_gy)}

    def greet(i, carry):
        pl.semaphore_signal(barrier, inc=1, device_id=peer_id(i), device_id_type=MESH)
        return carry

    lax.fori_loop(1, n, greet, 0)

    inner_x, inner_y = pl.ds(1, nx), pl.ds(TOP, ny)
    loads = {}

    def load(name, src, dst):
        copy = pltpu.make_async_copy(src, dst, load_sem.at[len(loads)])
        copy.start()
        loads[name] = copy

    load("traces", traces, rows)
    for g in range(2):
        for f in range(2):
            load(("now", g, f), fields[4 * g + 2 * f + 1], waves.at[g, 0, f, inner_x, inner_y])
    for i in range(5):
        load(("model", i), model[i], earth.at[i])
    for g in range(2):
        for f in range(2):
            load(("prev", g, f), fields[4 * g + 2 * f], olds.at[g, f])
    load("rx", rec_x, rec_pos.at[0])
    load("ry", rec_y, rec_pos.at[1])

    for edge, plane in ((gx == 0, 0), (gx == n_gx - 1, nx + 1)):
        @pl.when(edge)
        def _():
            for g in range(2):
                for level in range(STEPS):
                    for f in range(2):
                        waves[g, level, f, plane, TOP - 8:TOP + ny + 8] = jnp.zeros((ny + 16, nz), jnp.float32)
    for edge, row in ((gy == 0, TOP - 1), (gy == n_gy - 1, TOP + ny)):
        @pl.when(edge)
        def _():
            for g in range(2):
                for level in range(STEPS):
                    for f in range(2):
                        waves[g, level, f, :, row:row + 1] = jnp.zeros((nx + 2, 1, nz), jnp.float32)

    loads["traces"].wait()
    window[...] = jnp.zeros_like(window)
    window[0:STEPS, 0:local_rec] = rows[pl.ds(start[0], STEPS), :]

    def there(dx, dy):
        ok = None
        for d, pos, count in ((dx, gx, n_gx), (dy, gy, n_gy)):
            if d:
                test = pos + d < count if d > 0 else pos + d >= 0
                ok = test if ok is None else ok & test
        return ok

    def halo_copy(g, level, i):
        dx, dy = DIRS[i]
        src_x = {0: inner_x, 1: pl.ds(nx, 1), -1: pl.ds(1, 1)}[dx]
        dst_x = {0: inner_x, 1: pl.ds(0, 1), -1: pl.ds(nx + 1, 1)}[dx]
        src_y = {0: inner_y, 1: pl.ds(TOP + ny - 1, 1), -1: pl.ds(TOP, 1)}[dy]
        dst_y = {0: inner_y, 1: pl.ds(TOP - 1, 1), -1: pl.ds(TOP + ny, 1)}[dy]
        return pltpu.make_async_remote_copy(
            src_ref=waves.at[g, level, :, src_x, src_y],
            dst_ref=waves.at[g, level, :, dst_x, dst_y],
            send_sem=send_sem.at[g, level, i],
            recv_sem=recv_sem.at[g, level, i],
            device_id={"gx": gx + dx, "gy": gy + dy},
            device_id_type=MESH,
        )

    def send_halo(g, level):
        for i, (dx, dy) in enumerate(DIRS):
            @pl.when(there(dx, dy))
            def _():
                halo_copy(g, level, i).start()

    def await_halo(g, level):
        for i, (dx, dy) in enumerate(DIRS):
            @pl.when(there(-dx, -dy))
            def _():
                halo_copy(g, level, i).wait_recv()

    def finish_halo(g, level):
        for i, (dx, dy) in enumerate(DIRS):
            @pl.when(there(dx, dy))
            def _():
                halo_copy(g, level, i).wait_send()

    def far_copy(i):
        return pltpu.make_async_remote_copy(
            src_ref=window,
            dst_ref=gathered.at[me],
            send_sem=far_send.at[i],
            recv_sem=far_recv.at[me],
            device_id=peer_id(i),
            device_id_type=MESH,
        )

    def far_start(i, carry):
        far_copy(i).start()
        return carry

    def far_finish(i, carry):
        far_copy(i).wait_send()
        return carry

    def far_await(i, carry):
        peer = lax.rem(me + i, n)
        pltpu.make_async_remote_copy(
            src_ref=window,
            dst_ref=gathered.at[peer],
            send_sem=far_send.at[i],
            recv_sem=far_recv.at[peer],
            device_id=peer_id(i),
            device_id_type=MESH,
        ).wait_recv()
        return carry

    for g in range(2):
        for f in range(2):
            loads["now", g, f].wait()
    gathered[me] = window[...]
    pl.semaphore_wait(barrier, n - 1)
    send_halo(0, 0)
    lax.fori_loop(1, n, far_start, 0)
    send_halo(1, 0)

    for i in range(5):
        loads["model", i].wait()

    def factors(x, carry):
        v = earth[0, x]
        f_e = 1.0 + 2.0 * earth[1, x]
        f_d = jnp.sqrt(1.0 + 2.0 * earth[2, x])
        tilt = earth[3, x]
        half = 0.5 * earth[4, x]
        sin_t, cos_t = sine(tilt), cosine(tilt)
        sin_h, cos_h = sine(half), cosine(half)
        sin_a = 2.0 * sin_h * cos_h
        cos_a = 1.0 - 2.0 * sin_h * sin_h
        square = sin_t * sin_t
        twice = (0.5 * sin_t) * cos_t
        coef[0, x] = square * cos_a * cos_a
        coef[1, x] = square * sin_a * sin_a
        coef[2, x] = cos_t * cos_t
        coef[3, x] = (0.5 * square) * sin_a * cos_a
        coef[4, x] = twice * cos_a
        coef[5, x] = twice * sin_a
        coef[6, x] = v * f_e
        coef[7, x] = v * f_d
        return carry

    lax.fori_loop(0, nx, factors, 0, unroll=2)

    for g in range(2):
        for f in range(2):
            loads["prev", g, f].wait()
    loads["rx"].wait()
    loads["ry"].wait()

    lane = lax.broadcasted_iota(jnp.int32, (ny, nz), 1)
    first, last = lane == 0, lane == nz - 1

    def after(value):
        return jnp.where(last, 0.0, pltpu.roll(value, nz - 1, 1))

    def before(value):
        return jnp.where(first, 0.0, pltpu.roll(value, 1, 1))

    mid, up, down = pl.ds(TOP, ny), pl.ds(TOP + 1, ny), pl.ds(TOP - 1, ny)

    def rotated(now, f, x):
        center = now[f, x + 1, mid]
        x_up, x_down = now[f, x + 2, mid], now[f, x, mid]
        y_up, y_down = now[f, x + 1, up], now[f, x + 1, down]
        d_x, d_y = x_up - x_down, y_up - y_down
        s_x, s_y = x_up + x_down, y_up + y_down
        s_z = after(center) + before(center)
        d_xy = (now[f, x + 2, up] - now[f, x + 2, down]) - (now[f, x, up] - now[f, x, down])
        d_xz = after(d_x) - before(d_x)
        d_yz = after(d_y) - before(d_y)
        axis = (
            (coef[0, x] * s_x + coef[1, x] * s_y)
            + (coef[2, x] * s_z + coef[3, x] * d_xy)
            + (coef[4, x] * d_xz + coef[5, x] * d_yz)
        ) - 2.0 * center
        return center, axis, (s_x + s_y) + (s_z - 6.0 * center)

    def step(g, level):
        now = waves.at[g, level]

        def plane(x, carry):
            p_now, p_axis, laplace = rotated(now, 0, x)
            q_now, q_axis, _ = rotated(now, 1, x)
            across = laplace - p_axis
            if level == 0:
                p_prev, q_prev = olds[g, 0, x], olds[g, 1, x]
            else:
                p_prev, q_prev = waves[g, level - 1, 0, x + 1, mid], waves[g, level - 1, 1, x + 1, mid]
            v_d = coef[7, x]
            p_next = (2.0 * p_now - p_prev) + (coef[6, x] * across + v_d * q_axis)
            q_next = (2.0 * q_now - q_prev) + (v_d * across + earth[0, x] * q_axis)
            if g == 1:
                p_next = p_next + inject[STEPS - 1 - level, x]
            if g == 1 and level == STEPS - 1:
                p_last[x] = p_next
                q_last[x] = q_next
                total = waves[0, 0, 0, x + 1, mid] * p_next
                for k in range(STEPS):
                    total = total + waves[1, k, 0, x + 1, mid] * waves[0, STEPS - k, 0, x + 1, mid]
                image[x] = total
            else:
                waves[g, level + 1, 0, x + 1, mid] = p_next
                waves[g, level + 1, 1, x + 1, mid] = q_next
            return carry

        lax.fori_loop(0, nx, plane, 0, unroll=2)

    def make_planes():
        per_row = LANES // local_rec
        n_rows = n_rec // LANES
        chunk = min(8, n_rows)
        x_id = lax.broadcasted_iota(jnp.int32, (nx, LANES), 0) + gx * nx
        y_id = lax.broadcasted_iota(jnp.int32, (ny, LANES), 0) + gy * ny
        total = jnp.zeros((ny, STEPS * nx), jnp.float32)
        for base in range(0, n_rows, chunk):
            lefts, rights = [], []
            for i in range(base, base + chunk):
                sample = gathered[i * per_row]
                for j in range(1, per_row):
                    sample = sample + pltpu.roll(gathered[i * per_row + j], j * local_rec, 1)
                at_x = rec_pos[0, i:i + 1] == x_id
                lefts.append(jnp.where(rec_pos[1, i:i + 1] == y_id, 1.0, 0.0))
                rights.append(
                    jnp.concatenate(
                        [jnp.where(at_x, sample[k:k + 1], 0.0) for k in range(STEPS)], axis=0
                    )
                )
            total = total + lax.dot_general(
                jnp.concatenate(lefts, axis=1),
                jnp.concatenate(rights, axis=1),
                (((1,), (1,)), ((), ())),
                precision=lax.Precision.HIGHEST,
                preferred_element_type=jnp.float32,
            )
        here = lane == REC_DEPTH
        for k in range(STEPS):
            for x in range(nx):
                column = k * nx + x
                inject[k, x] = jnp.where(here, total[:, column:column + 1], 0.0)

    for level in range(STEPS):
        await_halo(0, level)
        step(0, level)
        if level < STEPS - 1:
            send_halo(0, level + 1)
        if level == 0:
            lax.fori_loop(1, n, far_await, 0)
            make_planes()
        await_halo(1, level)
        step(1, level)
        if level < STEPS - 1:
            send_halo(1, level + 1)
    lax.fori_loop(1, n, far_finish, 0)
    for level in range(STEPS):
        for g in range(2):
            finish_halo(g, level)


def per_device(*args):
    nx, ny, nz = args[0].shape
    n_gx, n_gy = lax.axis_size("gx"), lax.axis_size("gy")
    traces, receiver_x, receiver_y, segment_start = args[13:]
    samples, local_rec = traces.shape
    n_rec = receiver_x.shape[0]
    n = n_gx * n_gy
    sizes = (n_gx, n_gy, nx, ny, nz, local_rec, n_rec)
    positions = [r.reshape(n_rec // LANES, LANES) for r in (receiver_x, receiver_y)]
    anywhere = pl.BlockSpec(memory_space=pl.ANY)
    block = jax.ShapeDtypeStruct((nx, ny, nz), jnp.float32)
    return pl.pallas_call(
        functools.partial(kernel, sizes),
        out_shape=(block,) * 3,
        in_specs=[anywhere] * 16 + [pl.BlockSpec(memory_space=pltpu.SMEM)],
        out_specs=(pl.BlockSpec(memory_space=pltpu.VMEM),) * 3,
        scratch_shapes=[
            pltpu.VMEM((2, STEPS + 1, 2, nx + 2, ny + 16, nz), jnp.float32),
            pltpu.VMEM((2, 2, nx, ny, nz), jnp.float32),
            pltpu.VMEM((8, nx, ny, nz), jnp.float32),
            pltpu.VMEM((5, nx, ny, nz), jnp.float32),
            pltpu.VMEM((STEPS, nx, ny, nz), jnp.float32),
            pltpu.VMEM((samples, local_rec), jnp.float32),
            pltpu.VMEM((8, LANES), jnp.float32),
            pltpu.VMEM((n, 8, LANES), jnp.float32),
            pltpu.VMEM((2, n_rec // LANES, LANES), jnp.int32),
            pltpu.SemaphoreType.DMA((16,)),
            pltpu.SemaphoreType.DMA((2, STEPS, 8)),
            pltpu.SemaphoreType.DMA((2, STEPS, 8)),
            pltpu.SemaphoreType.DMA((n,)),
            pltpu.SemaphoreType.DMA((n,)),
        ],
        compiler_params=pltpu.CompilerParams(
            collective_id=0, has_side_effects=True, vmem_limit_bytes=48 * 1024 * 1024
        ),
        name="window",
    )(*args[:13], traces, *positions, segment_start)


def solution(mesh):
    block, cell = P(("shot", "gx"), "gy", None), P("gx", "gy", None)
    return jax.shard_map(
        per_device,
        mesh=mesh,
        in_specs=(block,) * 8 + (cell,) * 5 + (P("shot", ("gx", "gy")), P(), P(), P()),
        out_specs=(block,) * 3,
        check_vma=False,
    )
```

time: 142 us -> 42.5 us (0.30)
  starting transfers between devices: 39 us -> 0 us
  other arithmetic: 33.5 us -> 0 us
  blocking collectives: 28.7 us -> 0 us
  Pallas kernels: 0 us -> 25.6 us
  waiting for transfers between devices: 23.2 us -> 0 us
    ppermute x16 -> x0, starting transfers between devices: 39 us -> none  [the longest x8 26 us: padded_2(): before = lax.ppermute(last, axis, up)]
    all_gather x1 -> x0, blocking collectives: 28.7 us -> none  [per_device(): everyone = lax.all_gather(window, ('gx', 'gy'), axis=1, tiled=True)]
    pallas_call x0 -> x1, Pallas kernels: none -> 25.6 us  [per_device(): pl.pallas_call(functools.partial(kernel, sizes), out_shape=(block,) * 3,...]
    ppermute x16 -> x0, waiting for transfers between devices: 23.2 us -> none  [the longest x8 23.1 us: padded_2(): after = lax.ppermute(initial, axis, down)]
    mul x11 -> x0, other arithmetic: 16.5 us -> none  [the longest x2 8.05 us: rotated(): d_xx = padded[2:, 1:-1, 1:-1] - 2.0 * center + padded[:-2, 1:-1, 1:-1]]
    sub x3 -> x0, other arithmetic: 12.1 us -> none  [advance(): p_across = p_laplace - p_axis]
    unnamed x71 -> x35, local copies, waits for them, and re-layouts: 8.43 us -> 15.1 us
    scatter-add x4 -> x0, local copies, waits for them, and re-layouts: 5.78 us -> none  [run_round(): p_next = p_next.at[:, :, REC_DEPTH].add(planes[sample])]
  transfers between devices with their start and end apart: 16 -> 0, of which waited for: 7 -> 0; matrix products, arithmetic and copies ran while one was open for 1% -> 0% of each run, Pallas kernels for 0% -> 0%
where the time goes in v1:
time: 42.5 us; the launch traced here: 42 us
  Pallas kernels  25.6 us (60%)
  local copies, waits for them, and re-layouts  15.1 us (36%)
  between operations  1.33 us (3%)
    pallas_call x1, Pallas kernels, per_device(): pl.pallas_call(functools.partial(kernel, sizes), out_shape=(block,) * 3,...  25.6 us
    unnamed x35, local copies, waits for them, and re-layouts  15.1 us

profile of v1, /device:TPU:1, one launch (start us, length us, event | category | flops | bytes accessed | tf_op | source)
XLA Modules:
  0.0 42.0 jit_solution(9564802673300465691)
XLA Ops:
  0.6 0.0 copy-start.14
  1.3 0.0 copy-done.14
  1.3 0.0 copy-start
  1.3 0.9 %copy-done = f32[16,16,128]{2,1,0:T(8,128)S(1)} copy-done((f32[16,16,128]{2,1,0:T(8,128)S(1)}, f32[16,16,128]{2,1,0:T(8,128)}, u32[]{:S(2)}) %copy-start) | copy-done | bytes 131096
  2.2 0.0 copy-start.1
  2.2 0.9 %copy-done.1 = f32[16,16,128]{2,1,0:T(8,128)S(1)} copy-done((f32[16,16,128]{2,1,0:T(8,128)S(1)}, f32[16,16,128]{2,1,0:T(8,128)}, u32[]{:S(2)}) %copy-start.1) | copy-done | bytes 131096
  3.1 0.0 copy-start.2
  3.1 0.9 %copy-done.2 = f32[16,16,128]{2,1,0:T(8,128)S(1)} copy-done((f32[16,16,128]{2,1,0:T(8,128)S(1)}, f32[16,16,128]{2,1,0:T(8,128)}, u32[]{:S(2)}) %copy-start.2) | copy-done | bytes 131096
  4.0 0.9 %copy-done.3 = f32[16,16,128]{2,1,0:T(8,128)S(1)} copy-done((f32[16,16,128]{2,1,0:T(8,128)S(1)}, f32[16,16,128]{2,1,0:T(8,128)}, u32[]{:S(2)}) %copy-start.3) | copy-done | bytes 131096
  4.9 0.9 %copy-done.4 = f32[16,16,128]{2,1,0:T(8,128)S(1)} copy-done((f32[16,16,128]{2,1,0:T(8,128)S(1)}, f32[16,16,128]{2,1,0:T(8,128)}, u32[]{:S(2)}) %copy-start.4) | copy-done | bytes 131096
  5.9 0.9 %copy-done.5 = f32[16,16,128]{2,1,0:T(8,128)S(1)} copy-done((f32[16,16,128]{2,1,0:T(8,128)S(1)}, f32[16,16,128]{2,1,0:T(8,128)}, u32[]{:S(2)}) %copy-start.5) | copy-done | bytes 131096
  6.8 0.9 %copy-done.6 = f32[16,16,128]{2,1,0:T(8,128)S(1)} copy-done((f32[16,16,128]{2,1,0:T(8,128)S(1)}, f32[16,16,128]{2,1,0:T(8,128)}, u32[]{:S(2)}) %copy-start.6) | copy-done | bytes 131096
  7.7 0.9 %copy-done.7 = f32[16,16,128]{2,1,0:T(8,128)S(1)} copy-done((f32[16,16,128]{2,1,0:T(8,128)S(1)}, f32[16,16,128]{2,1,0:T(8,128)}, u32[]{:S(2)}) %copy-start.7) | copy-done | bytes 131096
  8.6 0.9 %copy-done.8 = f32[16,16,128]{2,1,0:T(8,128)S(1)} copy-done((f32[16,16,128]{2,1,0:T(8,128)S(1)}, f32[16,16,128]{2,1,0:T(8,128)}, u32[]{:S(2)}) %copy-start.8) | copy-done | bytes 131096
  9.5 0.9 %copy-done.9 = f32[16,16,128]{2,1,0:T(8,128)S(1)} copy-done((f32[16,16,128]{2,1,0:T(8,128)S(1)}, f32[16,16,128]{2,1,0:T(8,128)}, u32[]{:S(2)}) %copy-start.9) | copy-done | bytes 131096
  10.4 0.9 %copy-done.10 = f32[16,16,128]{2,1,0:T(8,128)S(1)} copy-done((f32[16,16,128]{2,1,0:T(8,128)S(1)}, f32[16,16,128]{2,1,0:T(8,128)}, u32[]{:S(2)}) %copy-start.10) | copy-done | bytes 131096
  11.3 0.9 %copy-done.11 = f32[16,16,128]{2,1,0:T(8,128)S(1)} copy-done((f32[16,16,128]{2,1,0:T(8,128)S(1)}, f32[16,16,128]{2,1,0:T(8,128)}, u32[]{:S(2)}) %copy-start.11) | copy-done | bytes 131096
  12.2 0.9 %copy-done.12 = f32[16,16,128]{2,1,0:T(8,128)S(1)} copy-done((f32[16,16,128]{2,1,0:T(8,128)S(1)}, f32[16,16,128]{2,1,0:T(8,128)}, u32[]{:S(2)}) %copy-start.12) | copy-done | bytes 131096
  13.1 0.7 %copy-done.13 = f32[16,64]{1,0:T(8,128)S(1)} copy-done((f32[16,64]{1,0:T(8,128)S(1)}, f32[16,64]{1,0:T(8,128)}, u32[]{:S(2)}) %copy-start.13) | copy-done | bytes 4120
  13.8 0.7 %copy-done.15 = s32[1024]{0:T(1024)S(1)} copy-done((s32[1024]{0:T(1024)S(1)}, s32[1024]{0:T(1024)}, u32[]{:S(2)}) %copy-start.15) | copy-done | bytes 4120
  14.5 25.6 %window.1 = (f32[16,16,128]{2,1,0:T(8,128)S(1)}, f32[16,16,128]{2,1,0:T(8,128)S(1)}, f32[16,16,128]{2,1,0:T(8,128)S(1)}) custom-call(f32[16,16,128]{2,1,0:T(8,128)S(1)} %copy-done, f32[16,16,128]{2,1,0:T(8,128)S(1)} %copy-done.1, f32[16,16,128]{2,1,0:T(8,128)S(1)} %copy-done.2, f32[16,16,128]{2,1,0:T(8,128)S(1)} %copy-done.3, f32[16,16,128]{2,1,0:T(8,128)S(1)} %copy-done.4, ...), custom_call_target="tpu_custom_call" | custom-call | tf_op jit(solution)/shard_map/window/pallas_call | solution.py:330
  40.1 0.7 %copy.24 = f32[16,16,128]{2,1,0:T(8,128)} copy(f32[16,16,128]{2,1,0:T(8,128)S(1)} %get-tuple-element.6) | data formatting | bytes 262144
  40.7 0.7 %copy.25 = f32[16,16,128]{2,1,0:T(8,128)} copy(f32[16,16,128]{2,1,0:T(8,128)S(1)} %get-tuple-element.7) | data formatting | bytes 262144
  41.4 0.7 %copy.26 = f32[16,16,128]{2,1,0:T(8,128)} copy(f32[16,16,128]{2,1,0:T(8,128)S(1)} %get-tuple-element.8) | data formatting | bytes 262144
  (12 shorter events, 0.0 us)
Async XLA Ops:
  0.6 0.7 %copy-start.14 = (s32[1024]{0:T(1024)S(1)}, s32[1024]{0:T(1024)}, u32[]{:S(2)}) copy-start(s32[1024]{0:T(1024)} %param.31) | copy-start | bytes 12292
  1.3 0.9 %copy-start = (f32[16,16,128]{2,1,0:T(8,128)S(1)}, f32[16,16,128]{2,1,0:T(8,128)}, u32[]{:S(2)}) copy-start(f32[16,16,128]{2,1,0:T(8,128)} %refs_0_.1) | copy-start | bytes 393220
  2.2 0.9 %copy-start.1 = (f32[16,16,128]{2,1,0:T(8,128)S(1)}, f32[16,16,128]{2,1,0:T(8,128)}, u32[]{:S(2)}) copy-start(f32[16,16,128]{2,1,0:T(8,128)} %refs_1_.1) | copy-start | bytes 393220
  3.1 0.9 %copy-start.2 = (f32[16,16,128]{2,1,0:T(8,128)S(1)}, f32[16,16,128]{2,1,0:T(8,128)}, u32[]{:S(2)}) copy-start(f32[16,16,128]{2,1,0:T(8,128)} %refs_2_.1) | copy-start | bytes 393220
  4.0 0.9 %copy-start.3 = (f32[16,16,128]{2,1,0:T(8,128)S(1)}, f32[16,16,128]{2,1,0:T(8,128)}, u32[]{:S(2)}) copy-start(f32[16,16,128]{2,1,0:T(8,128)} %refs_3_.1) | copy-start | bytes 393220
  4.9 0.9 %copy-start.4 = (f32[16,16,128]{2,1,0:T(8,128)S(1)}, f32[16,16,128]{2,1,0:T(8,128)}, u32[]{:S(2)}) copy-start(f32[16,16,128]{2,1,0:T(8,128)} %refs_4_.1) | copy-start | bytes 393220
  5.8 0.9 %copy-start.5 = (f32[16,16,128]{2,1,0:T(8,128)S(1)}, f32[16,16,128]{2,1,0:T(8,128)}, u32[]{:S(2)}) copy-start(f32[16,16,128]{2,1,0:T(8,128)} %refs_5_.1) | copy-start | bytes 393220
  6.8 0.9 %copy-start.6 = (f32[16,16,128]{2,1,0:T(8,128)S(1)}, f32[16,16,128]{2,1,0:T(8,128)}, u32[]{:S(2)}) copy-start(f32[16,16,128]{2,1,0:T(8,128)} %refs_6_.1) | copy-start | bytes 393220
  7.7 0.9 %copy-start.7 = (f32[16,16,128]{2,1,0:T(8,128)S(1)}, f32[16,16,128]{2,1,0:T(8,128)}, u32[]{:S(2)}) copy-start(f32[16,16,128]{2,1,0:T(8,128)} %refs_7_.1) | copy-start | bytes 393220
  8.6 0.9 %copy-start.8 = (f32[16,16,128]{2,1,0:T(8,128)S(1)}, f32[16,16,128]{2,1,0:T(8,128)}, u32[]{:S(2)}) copy-start(f32[16,16,128]{2,1,0:T(8,128)} %refs_8_.1) | copy-start | bytes 393220
  9.5 0.9 %copy-start.9 = (f32[16,16,128]{2,1,0:T(8,128)S(1)}, f32[16,16,128]{2,1,0:T(8,128)}, u32[]{:S(2)}) copy-start(f32[16,16,128]{2,1,0:T(8,128)} %refs_9_.1) | copy-start | bytes 393220
  10.4 0.9 %copy-start.10 = (f32[16,16,128]{2,1,0:T(8,128)S(1)}, f32[16,16,128]{2,1,0:T(8,128)}, u32[]{:S(2)}) copy-start(f32[16,16,128]{2,1,0:T(8,128)} %refs_10_.1) | copy-start | bytes 393220
  11.3 0.9 %copy-start.11 = (f32[16,16,128]{2,1,0:T(8,128)S(1)}, f32[16,16,128]{2,1,0:T(8,128)}, u32[]{:S(2)}) copy-start(f32[16,16,128]{2,1,0:T(8,128)} %refs_11_.1) | copy-start | bytes 393220
  12.2 0.9 %copy-start.12 = (f32[16,16,128]{2,1,0:T(8,128)S(1)}, f32[16,16,128]{2,1,0:T(8,128)}, u32[]{:S(2)}) copy-start(f32[16,16,128]{2,1,0:T(8,128)} %refs_12_.1) | copy-start | bytes 393220
  13.1 0.7 %copy-start.13 = (f32[16,64]{1,0:T(8,128)S(1)}, f32[16,64]{1,0:T(8,128)}, u32[]{:S(2)}) copy-start(f32[16,64]{1,0:T(8,128)} %refs_13_.1) | copy-start | bytes 12292
  13.8 0.7 %copy-start.15 = (s32[1024]{0:T(1024)S(1)}, s32[1024]{0:T(1024)}, u32[]{:S(2)}) copy-start(s32[1024]{0:T(1024)} %param.32) | copy-start | bytes 12292

commit v2 on v1

--- a/solution.py
+++ b/solution.py
@@ -325,7 +325,7 @@
     n = n_gx * n_gy
     sizes = (n_gx, n_gy, nx, ny, nz, local_rec, n_rec)
     positions = [r.reshape(n_rec // LANES, LANES) for r in (receiver_x, receiver_y)]
-    anywhere = pl.BlockSpec(memory_space=pl.ANY)
+    anywhere = pl.BlockSpec(memory_space=pltpu.HBM)
     block = jax.ShapeDtypeStruct((nx, ny, nz), jnp.float32)
     return pl.pallas_call(
         functools.partial(kernel, sizes),

time: 42.5 us -> 42.5 us (level)
  no operation moved by 1% of the time
where the time goes in v2:
time: 42.5 us; the launch traced here: 42 us
  Pallas kernels  25.6 us (60%)
  local copies, waits for them, and re-layouts  15.1 us (36%)
  between operations  1.33 us (3%)
    pallas_call x1, Pallas kernels, per_device(): pl.pallas_call(functools.partial(kernel, sizes), out_shape=(block,) * 3,...  25.6 us
    unnamed x35, local copies, waits for them, and re-layouts  15.1 us

profile of v2, /device:TPU:1, one launch (start us, length us, event | category | flops | bytes accessed | tf_op | source)
XLA Modules:
  0.0 42.0 jit_solution(9564802673300465691)
XLA Ops:
  0.6 0.0 copy-start.14
  1.3 0.0 copy-done.14
  1.3 0.0 copy-start
  1.3 0.9 %copy-done = f32[16,16,128]{2,1,0:T(8,128)S(1)} copy-done((f32[16,16,128]{2,1,0:T(8,128)S(1)}, f32[16,16,128]{2,1,0:T(8,128)}, u32[]{:S(2)}) %copy-start) | copy-done | bytes 131096
  2.2 0.0 copy-start.1
  2.2 0.9 %copy-done.1 = f32[16,16,128]{2,1,0:T(8,128)S(1)} copy-done((f32[16,16,128]{2,1,0:T(8,128)S(1)}, f32[16,16,128]{2,1,0:T(8,128)}, u32[]{:S(2)}) %copy-start.1) | copy-done | bytes 131096
  3.1 0.0 copy-start.2
  3.1 0.9 %copy-done.2 = f32[16,16,128]{2,1,0:T(8,128)S(1)} copy-done((f32[16,16,128]{2,1,0:T(8,128)S(1)}, f32[16,16,128]{2,1,0:T(8,128)}, u32[]{:S(2)}) %copy-start.2) | copy-done | bytes 131096
  4.0 0.9 %copy-done.3 = f32[16,16,128]{2,1,0:T(8,128)S(1)} copy-done((f32[16,16,128]{2,1,0:T(8,128)S(1)}, f32[16,16,128]{2,1,0:T(8,128)}, u32[]{:S(2)}) %copy-start.3) | copy-done | bytes 131096
  4.9 0.9 %copy-done.4 = f32[16,16,128]{2,1,0:T(8,128)S(1)} copy-done((f32[16,16,128]{2,1,0:T(8,128)S(1)}, f32[16,16,128]{2,1,0:T(8,128)}, u32[]{:S(2)}) %copy-start.4) | copy-done | bytes 131096
  5.9 0.9 %copy-done.5 = f32[16,16,128]{2,1,0:T(8,128)S(1)} copy-done((f32[16,16,128]{2,1,0:T(8,128)S(1)}, f32[16,16,128]{2,1,0:T(8,128)}, u32[]{:S(2)}) %copy-start.5) | copy-done | bytes 131096
  6.8 0.9 %copy-done.6 = f32[16,16,128]{2,1,0:T(8,128)S(1)} copy-done((f32[16,16,128]{2,1,0:T(8,128)S(1)}, f32[16,16,128]{2,1,0:T(8,128)}, u32[]{:S(2)}) %copy-start.6) | copy-done | bytes 131096
  7.7 0.9 %copy-done.7 = f32[16,16,128]{2,1,0:T(8,128)S(1)} copy-done((f32[16,16,128]{2,1,0:T(8,128)S(1)}, f32[16,16,128]{2,1,0:T(8,128)}, u32[]{:S(2)}) %copy-start.7) | copy-done | bytes 131096
  8.6 0.9 %copy-done.8 = f32[16,16,128]{2,1,0:T(8,128)S(1)} copy-done((f32[16,16,128]{2,1,0:T(8,128)S(1)}, f32[16,16,128]{2,1,0:T(8,128)}, u32[]{:S(2)}) %copy-start.8) | copy-done | bytes 131096
  9.5 0.9 %copy-done.9 = f32[16,16,128]{2,1,0:T(8,128)S(1)} copy-done((f32[16,16,128]{2,1,0:T(8,128)S(1)}, f32[16,16,128]{2,1,0:T(8,128)}, u32[]{:S(2)}) %copy-start.9) | copy-done | bytes 131096
  10.4 0.9 %copy-done.10 = f32[16,16,128]{2,1,0:T(8,128)S(1)} copy-done((f32[16,16,128]{2,1,0:T(8,128)S(1)}, f32[16,16,128]{2,1,0:T(8,128)}, u32[]{:S(2)}) %copy-start.10) | copy-done | bytes 131096
  11.3 0.9 %copy-done.11 = f32[16,16,128]{2,1,0:T(8,128)S(1)} copy-done((f32[16,16,128]{2,1,0:T(8,128)S(1)}, f32[16,16,128]{2,1,0:T(8,128)}, u32[]{:S(2)}) %copy-start.11) | copy-done | bytes 131096
  12.2 0.9 %copy-done.12 = f32[16,16,128]{2,1,0:T(8,128)S(1)} copy-done((f32[16,16,128]{2,1,0:T(8,128)S(1)}, f32[16,16,128]{2,1,0:T(8,128)}, u32[]{:S(2)}) %copy-start.12) | copy-done | bytes 131096
  13.1 0.7 %copy-done.13 = f32[16,64]{1,0:T(8,128)S(1)} copy-done((f32[16,64]{1,0:T(8,128)S(1)}, f32[16,64]{1,0:T(8,128)}, u32[]{:S(2)}) %copy-start.13) | copy-done | bytes 4120
  13.8 0.7 %copy-done.15 = s32[1024]{0:T(1024)S(1)} copy-done((s32[1024]{0:T(1024)S(1)}, s32[1024]{0:T(1024)}, u32[]{:S(2)}) %copy-start.15) | copy-done | bytes 4120
  14.5 25.6 %window.1 = (f32[16,16,128]{2,1,0:T(8,128)S(1)}, f32[16,16,128]{2,1,0:T(8,128)S(1)}, f32[16,16,128]{2,1,0:T(8,128)S(1)}) custom-call(f32[16,16,128]{2,1,0:T(8,128)S(1)} %copy-done, f32[16,16,128]{2,1,0:T(8,128)S(1)} %copy-done.1, f32[16,16,128]{2,1,0:T(8,128)S(1)} %copy-done.2, f32[16,16,128]{2,1,0:T(8,128)S(1)} %copy-done.3, f32[16,16,128]{2,1,0:T(8,128)S(1)} %copy-done.4, ...), custom_call_target="tpu_custom_call" | custom-call | tf_op jit(solution)/shard_map/window/pallas_call | solution.py:330
  40.1 0.7 %copy.24 = f32[16,16,128]{2,1,0:T(8,128)} copy(f32[16,16,128]{2,1,0:T(8,128)S(1)} %get-tuple-element.6) | data formatting | bytes 262144
  40.7 0.7 %copy.25 = f32[16,16,128]{2,1,0:T(8,128)} copy(f32[16,16,128]{2,1,0:T(8,128)S(1)} %get-tuple-element.7) | data formatting | bytes 262144
  41.4 0.7 %copy.26 = f32[16,16,128]{2,1,0:T(8,128)} copy(f32[16,16,128]{2,1,0:T(8,128)S(1)} %get-tuple-element.8) | data formatting | bytes 262144
  (12 shorter events, 0.0 us)
Async XLA Ops:
  0.6 0.7 %copy-start.14 = (s32[1024]{0:T(1024)S(1)}, s32[1024]{0:T(1024)}, u32[]{:S(2)}) copy-start(s32[1024]{0:T(1024)} %param.31) | copy-start | bytes 12292
  1.3 0.9 %copy-start = (f32[16,16,128]{2,1,0:T(8,128)S(1)}, f32[16,16,128]{2,1,0:T(8,128)}, u32[]{:S(2)}) copy-start(f32[16,16,128]{2,1,0:T(8,128)} %refs_0_.1) | copy-start | bytes 393220
  2.2 0.9 %copy-start.1 = (f32[16,16,128]{2,1,0:T(8,128)S(1)}, f32[16,16,128]{2,1,0:T(8,128)}, u32[]{:S(2)}) copy-start(f32[16,16,128]{2,1,0:T(8,128)} %refs_1_.1) | copy-start | bytes 393220
  3.1 0.9 %copy-start.2 = (f32[16,16,128]{2,1,0:T(8,128)S(1)}, f32[16,16,128]{2,1,0:T(8,128)}, u32[]{:S(2)}) copy-start(f32[16,16,128]{2,1,0:T(8,128)} %refs_2_.1) | copy-start | bytes 393220
  4.0 0.9 %copy-start.3 = (f32[16,16,128]{2,1,0:T(8,128)S(1)}, f32[16,16,128]{2,1,0:T(8,128)}, u32[]{:S(2)}) copy-start(f32[16,16,128]{2,1,0:T(8,128)} %refs_3_.1) | copy-start | bytes 393220
  4.9 0.9 %copy-start.4 = (f32[16,16,128]{2,1,0:T(8,128)S(1)}, f32[16,16,128]{2,1,0:T(8,128)}, u32[]{:S(2)}) copy-start(f32[16,16,128]{2,1,0:T(8,128)} %refs_4_.1) | copy-start | bytes 393220
  5.8 0.9 %copy-start.5 = (f32[16,16,128]{2,1,0:T(8,128)S(1)}, f32[16,16,128]{2,1,0:T(8,128)}, u32[]{:S(2)}) copy-start(f32[16,16,128]{2,1,0:T(8,128)} %refs_5_.1) | copy-start | bytes 393220
  6.8 0.9 %copy-start.6 = (f32[16,16,128]{2,1,0:T(8,128)S(1)}, f32[16,16,128]{2,1,0:T(8,128)}, u32[]{:S(2)}) copy-start(f32[16,16,128]{2,1,0:T(8,128)} %refs_6_.1) | copy-start | bytes 393220
  7.7 0.9 %copy-start.7 = (f32[16,16,128]{2,1,0:T(8,128)S(1)}, f32[16,16,128]{2,1,0:T(8,128)}, u32[]{:S(2)}) copy-start(f32[16,16,128]{2,1,0:T(8,128)} %refs_7_.1) | copy-start | bytes 393220
  8.6 0.9 %copy-start.8 = (f32[16,16,128]{2,1,0:T(8,128)S(1)}, f32[16,16,128]{2,1,0:T(8,128)}, u32[]{:S(2)}) copy-start(f32[16,16,128]{2,1,0:T(8,128)} %refs_8_.1) | copy-start | bytes 393220
  9.5 0.9 %copy-start.9 = (f32[16,16,128]{2,1,0:T(8,128)S(1)}, f32[16,16,128]{2,1,0:T(8,128)}, u32[]{:S(2)}) copy-start(f32[16,16,128]{2,1,0:T(8,128)} %refs_9_.1) | copy-start | bytes 393220
  10.4 0.9 %copy-start.10 = (f32[16,16,128]{2,1,0:T(8,128)S(1)}, f32[16,16,128]{2,1,0:T(8,128)}, u32[]{:S(2)}) copy-start(f32[16,16,128]{2,1,0:T(8,128)} %refs_10_.1) | copy-start | bytes 393220
  11.3 0.9 %copy-start.11 = (f32[16,16,128]{2,1,0:T(8,128)S(1)}, f32[16,16,128]{2,1,0:T(8,128)}, u32[]{:S(2)}) copy-start(f32[16,16,128]{2,1,0:T(8,128)} %refs_11_.1) | copy-start | bytes 393220
  12.2 0.9 %copy-start.12 = (f32[16,16,128]{2,1,0:T(8,128)S(1)}, f32[16,16,128]{2,1,0:T(8,128)}, u32[]{:S(2)}) copy-start(f32[16,16,128]{2,1,0:T(8,128)} %refs_12_.1) | copy-start | bytes 393220
  13.1 0.7 %copy-start.13 = (f32[16,64]{1,0:T(8,128)S(1)}, f32[16,64]{1,0:T(8,128)}, u32[]{:S(2)}) copy-start(f32[16,64]{1,0:T(8,128)} %refs_13_.1) | copy-start | bytes 12292
  13.8 0.7 %copy-start.15 = (s32[1024]{0:T(1024)S(1)}, s32[1024]{0:T(1024)}, u32[]{:S(2)}) copy-start(s32[1024]{0:T(1024)} %param.32) | copy-start | bytes 12292

commit v3 on v2

--- a/solution.py
+++ b/solution.py
@@ -352,7 +352,7 @@
             collective_id=0, has_side_effects=True, vmem_limit_bytes=48 * 1024 * 1024
         ),
         name="window",
-    )(*args[:13], traces, *positions, segment_start)
+    )(*[pltpu.with_memory_space_constraint(a, pltpu.HBM) for a in (*args[:13], traces, *positions)], segment_start)
 
 
 def solution(mesh):

time: 42.5 us -> 29.3 us (0.69)
  local copies, waits for them, and re-layouts: 15.1 us -> 1.97 us
    unnamed x35 -> x3, local copies, waits for them, and re-layouts: 15.1 us -> 1.97 us
where the time goes in v3:
time: 29.3 us; the launch traced here: 29.1 us
  Pallas kernels  25.8 us (88%)
  local copies, waits for them, and re-layouts  1.97 us (7%)
  between operations  1.29 us (4%)
    pallas_call x1, Pallas kernels, per_device(): pl.pallas_call(functools.partial(kernel, sizes), out_shape=(block,) * 3,...  25.8 us
    unnamed x3, local copies, waits for them, and re-layouts  1.97 us

profile of v3, /device:TPU:1, one launch (start us, length us, event | category | flops | bytes accessed | tf_op | source)
XLA Modules:
  0.0 29.1 jit_solution(17688007573850165995)
XLA Ops:
  1.3 25.8 %window.1 = (f32[16,16,128]{2,1,0:T(8,128)S(1)}, f32[16,16,128]{2,1,0:T(8,128)S(1)}, f32[16,16,128]{2,1,0:T(8,128)S(1)}) custom-call(f32[16,16,128]{2,1,0:T(8,128)} %refs_0_.1, f32[16,16,128]{2,1,0:T(8,128)} %refs_1_.1, f32[16,16,128]{2,1,0:T(8,128)} %refs_2_.1, f32[16,16,128]{2,1,0:T(8,128)} %refs_3_.1, f32[16,16,128]{2,1,0:T(8,128)} %refs_4_.1, ...), custom_call_target="tpu_custom_call" | custom-call | tf_op jit(solution)/shard_map/window/pallas_call | solution.py:330
  27.1 0.7 %copy.24 = f32[16,16,128]{2,1,0:T(8,128)} copy(f32[16,16,128]{2,1,0:T(8,128)S(1)} %get-tuple-element.6) | data formatting | bytes 262144
  27.8 0.7 %copy.25 = f32[16,16,128]{2,1,0:T(8,128)} copy(f32[16,16,128]{2,1,0:T(8,128)S(1)} %get-tuple-element.7) | data formatting | bytes 262144
  28.4 0.7 %copy.26 = f32[16,16,128]{2,1,0:T(8,128)} copy(f32[16,16,128]{2,1,0:T(8,128)S(1)} %get-tuple-element.8) | data formatting | bytes 262144

commit v4 on v3

--- a/solution.py
+++ b/solution.py
@@ -37,8 +37,9 @@
     fields, model = refs[:8], refs[8:13]
     traces, rec_x, rec_y, start = refs[13:17]
     image, p_last, q_last = refs[17:20]
-    (waves, olds, coef, earth, inject, rows, window, gathered, rec_pos,
+    (*held, olds, coef, earth, inject, rows, window, gathered, rec_pos,
      load_sem, send_sem, recv_sem, far_send, far_recv) = refs[20:]
+    waves = (held[:STEPS + 1], held[STEPS + 1:])
     n = n_gx * n_gy
     gx, gy = lax.axis_index("gx"), lax.axis_index("gy")
     me = gx * n_gy + gy
@@ -66,7 +67,7 @@
     load("traces", traces, rows)
     for g in range(2):
         for f in range(2):
-            load(("now", g, f), fields[4 * g + 2 * f + 1], waves.at[g, 0, f, inner_x, inner_y])
+            load(("now", g, f), fields[4 * g + 2 * f + 1], waves[g][0].at[f, inner_x, inner_y])
     for i in range(5):
         load(("model", i), model[i], earth.at[i])
     for g in range(2):
@@ -81,14 +82,14 @@
             for g in range(2):
                 for level in range(STEPS):
                     for f in range(2):
-                        waves[g, level, f, plane, TOP - 8:TOP + ny + 8] = jnp.zeros((ny + 16, nz), jnp.float32)
+                        waves[g][level][f, plane, TOP - 8:TOP + ny + 8] = jnp.zeros((ny + 16, nz), jnp.float32)
     for edge, row in ((gy == 0, TOP - 1), (gy == n_gy - 1, TOP + ny)):
         @pl.when(edge)
         def _():
             for g in range(2):
                 for level in range(STEPS):
                     for f in range(2):
-                        waves[g, level, f, :, row:row + 1] = jnp.zeros((nx + 2, 1, nz), jnp.float32)
+                        waves[g][level][f, :, row:row + 1] = jnp.zeros((nx + 2, 1, nz), jnp.float32)
 
     loads["traces"].wait()
     window[...] = jnp.zeros_like(window)
@@ -109,8 +110,8 @@
         src_y = {0: inner_y, 1: pl.ds(TOP + ny - 1, 1), -1: pl.ds(TOP, 1)}[dy]
         dst_y = {0: inner_y, 1: pl.ds(TOP - 1, 1), -1: pl.ds(TOP + ny, 1)}[dy]
         return pltpu.make_async_remote_copy(
-            src_ref=waves.at[g, level, :, src_x, src_y],
-            dst_ref=waves.at[g, level, :, dst_x, dst_y],
+            src_ref=waves[g][level].at[:, src_x, src_y],
+            dst_ref=waves[g][level].at[:, dst_x, dst_y],
             send_sem=send_sem.at[g, level, i],
             recv_sem=recv_sem.at[g, level, i],
             device_id={"gx": gx + dx, "gy": gy + dy},
@@ -176,6 +177,15 @@
 
     for i in range(5):
         loads["model", i].wait()
+
+    lane = lax.broadcasted_iota(jnp.int32, (ny, nz), 1)
+    first, last = lane == 0, lane == nz - 1
+
+    def after(value):
+        return pltpu.roll(value, nz - 1, 1)
+
+    def before(value):
+        return pltpu.roll(value, 1, 1)
 
     def factors(x, carry):
         v = earth[0, x]
@@ -189,17 +199,26 @@
         cos_a = 1.0 - 2.0 * sin_h * sin_h
         square = sin_t * sin_t
         twice = (0.5 * sin_t) * cos_t
-        coef[0, x] = square * cos_a * cos_a
-        coef[1, x] = square * sin_a * sin_a
-        coef[2, x] = cos_t * cos_t
-        coef[3, x] = (0.5 * square) * sin_a * cos_a
-        coef[4, x] = twice * cos_a
-        coef[5, x] = twice * sin_a
-        coef[6, x] = v * f_e
-        coef[7, x] = v * f_d
-        return carry
-
-    lax.fori_loop(0, nx, factors, 0, unroll=2)
+        a_xx = square * cos_a * cos_a
+        a_yy = square * sin_a * sin_a
+        a_zz = cos_t * cos_t
+        a_xz, a_yz = twice * cos_a, twice * sin_a
+        coef[0, x] = a_xx
+        coef[1, x] = a_yy
+        coef[4, x] = 1.0 - a_xx
+        coef[5, x] = 1.0 - a_yy
+        coef[8, x] = (0.5 * square) * sin_a * cos_a
+        for shift, edge, i in ((before, first, 0), (after, last, 1)):
+            moved = shift(a_zz)
+            coef[2 + i, x] = jnp.where(edge, 0.0, moved)
+            coef[6 + i, x] = jnp.where(edge, 0.0, 1.0 - moved)
+            coef[9 + 2 * i, x] = jnp.where(edge, 0.0, shift(a_xz))
+            coef[10 + 2 * i, x] = jnp.where(edge, 0.0, shift(a_yz))
+        coef[13, x] = v * f_e
+        coef[14, x] = v * f_d
+        return carry
+
+    lax.fori_loop(0, nx, factors, 0, unroll=4)
 
     for g in range(2):
         for f in range(2):
@@ -207,63 +226,53 @@
     loads["rx"].wait()
     loads["ry"].wait()
 
-    lane = lax.broadcasted_iota(jnp.int32, (ny, nz), 1)
-    first, last = lane == 0, lane == nz - 1
-
-    def after(value):
-        return jnp.where(last, 0.0, pltpu.roll(value, nz - 1, 1))
-
-    def before(value):
-        return jnp.where(first, 0.0, pltpu.roll(value, 1, 1))
-
     mid, up, down = pl.ds(TOP, ny), pl.ds(TOP + 1, ny), pl.ds(TOP - 1, ny)
 
-    def rotated(now, f, x):
-        center = now[f, x + 1, mid]
+    def rotated(now, f, x, center, weights):
+        sign, w_x, w_y, w_up, w_down = weights
         x_up, x_down = now[f, x + 2, mid], now[f, x, mid]
         y_up, y_down = now[f, x + 1, up], now[f, x + 1, down]
         d_x, d_y = x_up - x_down, y_up - y_down
-        s_x, s_y = x_up + x_down, y_up + y_down
-        s_z = after(center) + before(center)
         d_xy = (now[f, x + 2, up] - now[f, x + 2, down]) - (now[f, x, up] - now[f, x, down])
-        d_xz = after(d_x) - before(d_x)
-        d_yz = after(d_y) - before(d_y)
-        axis = (
-            (coef[0, x] * s_x + coef[1, x] * s_y)
-            + (coef[2, x] * s_z + coef[3, x] * d_xy)
-            + (coef[4, x] * d_xz + coef[5, x] * d_yz)
-        ) - 2.0 * center
-        return center, axis, (s_x + s_y) + (s_z - 6.0 * center)
+        flat = coef[w_x, x] * (x_up + x_down) + coef[w_y, x] * (y_up + y_down)
+        mixed = coef[8, x] * d_xy
+        above, below = coef[w_up, x] * center, coef[w_down, x] * center
+        mixed_above = coef[9, x] * d_x + coef[10, x] * d_y
+        mixed_below = coef[11, x] * d_x + coef[12, x] * d_y
+        if sign > 0:
+            return (flat + mixed) + (after(above + mixed_above) + before(below - mixed_below))
+        return (flat - mixed) + (after(above - mixed_above) + before(below + mixed_below))
 
     def step(g, level):
-        now = waves.at[g, level]
+        now = waves[g][level]
 
         def plane(x, carry):
-            p_now, p_axis, laplace = rotated(now, 0, x)
-            q_now, q_axis, _ = rotated(now, 1, x)
-            across = laplace - p_axis
+            p_now, q_now = now[0, x + 1, mid], now[1, x + 1, mid]
+            p_two, q_two = p_now + p_now, q_now + q_now
+            across = rotated(now, 0, x, p_now, (-1, 4, 5, 6, 7)) - (p_two + p_two)
+            q_axis = rotated(now, 1, x, q_now, (1, 0, 1, 2, 3)) - q_two
             if level == 0:
                 p_prev, q_prev = olds[g, 0, x], olds[g, 1, x]
             else:
-                p_prev, q_prev = waves[g, level - 1, 0, x + 1, mid], waves[g, level - 1, 1, x + 1, mid]
-            v_d = coef[7, x]
-            p_next = (2.0 * p_now - p_prev) + (coef[6, x] * across + v_d * q_axis)
-            q_next = (2.0 * q_now - q_prev) + (v_d * across + earth[0, x] * q_axis)
+                p_prev, q_prev = waves[g][level - 1][0, x + 1, mid], waves[g][level - 1][1, x + 1, mid]
+            v_d = coef[14, x]
+            p_next = (p_two - p_prev) + (coef[13, x] * across + v_d * q_axis)
+            q_next = (q_two - q_prev) + (v_d * across + earth[0, x] * q_axis)
             if g == 1:
                 p_next = p_next + inject[STEPS - 1 - level, x]
             if g == 1 and level == STEPS - 1:
                 p_last[x] = p_next
                 q_last[x] = q_next
-                total = waves[0, 0, 0, x + 1, mid] * p_next
+                total = waves[0][0][0, x + 1, mid] * p_next
                 for k in range(STEPS):
-                    total = total + waves[1, k, 0, x + 1, mid] * waves[0, STEPS - k, 0, x + 1, mid]
+                    total = total + waves[1][k][0, x + 1, mid] * waves[0][STEPS - k][0, x + 1, mid]
                 image[x] = total
             else:
-                waves[g, level + 1, 0, x + 1, mid] = p_next
-                waves[g, level + 1, 1, x + 1, mid] = q_next
+                waves[g][level + 1][0, x + 1, mid] = p_next
+                waves[g][level + 1][1, x + 1, mid] = q_next
             return carry
 
-        lax.fori_loop(0, nx, plane, 0, unroll=2)
+        lax.fori_loop(0, nx, plane, 0, unroll=8)
 
     def make_planes():
         per_row = LANES // local_rec
@@ -333,9 +342,9 @@
         in_specs=[anywhere] * 16 + [pl.BlockSpec(memory_space=pltpu.SMEM)],
         out_specs=(pl.BlockSpec(memory_space=pltpu.VMEM),) * 3,
         scratch_shapes=[
-            pltpu.VMEM((2, STEPS + 1, 2, nx + 2, ny + 16, nz), jnp.float32),
+            *[pltpu.VMEM((2, nx + 2, ny + 16, nz), jnp.float32)] * (2 * STEPS + 2),
             pltpu.VMEM((2, 2, nx, ny, nz), jnp.float32),
-            pltpu.VMEM((8, nx, ny, nz), jnp.float32),
+            pltpu.VMEM((15, nx, ny, nz), jnp.float32),
             pltpu.VMEM((5, nx, ny, nz), jnp.float32),
             pltpu.VMEM((STEPS, nx, ny, nz), jnp.float32),
             pltpu.VMEM((samples, local_rec), jnp.float32),

time: 29.3 us -> 26.6 us (0.908)
  Pallas kernels: 25.8 us -> 23.1 us
    pallas_call x1, Pallas kernels: 25.8 us -> 23.1 us  [per_device(): pl.pallas_call(functools.partial(kernel, sizes), out_shape=(block,) * 3,...]
where the time goes in v4:
time: 26.6 us; the launch traced here: 26.4 us
  Pallas kernels  23.1 us (87%)
  local copies, waits for them, and re-layouts  1.97 us (7%)
  between operations  1.29 us (5%)
    pallas_call x1, Pallas kernels, per_device(): pl.pallas_call(functools.partial(kernel, sizes), out_shape=(block,) * 3,...  23.1 us
    unnamed x3, local copies, waits for them, and re-layouts  1.97 us

profile of v4, /device:TPU:1, one launch (start us, length us, event | category | flops | bytes accessed | tf_op | source)
XLA Modules:
  0.0 26.4 jit_solution(5319531079791145495)
XLA Ops:
  1.3 23.1 %window.1 = (f32[16,16,128]{2,1,0:T(8,128)S(1)}, f32[16,16,128]{2,1,0:T(8,128)S(1)}, f32[16,16,128]{2,1,0:T(8,128)S(1)}) custom-call(f32[16,16,128]{2,1,0:T(8,128)} %refs_0_.1, f32[16,16,128]{2,1,0:T(8,128)} %refs_1_.1, f32[16,16,128]{2,1,0:T(8,128)} %refs_2_.1, f32[16,16,128]{2,1,0:T(8,128)} %refs_3_.1, f32[16,16,128]{2,1,0:T(8,128)} %refs_4_.1, ...), custom_call_target="tpu_custom_call" | custom-call | tf_op jit(solution)/shard_map/window/pallas_call | solution.py:339
  24.4 0.7 %copy.24 = f32[16,16,128]{2,1,0:T(8,128)} copy(f32[16,16,128]{2,1,0:T(8,128)S(1)} %get-tuple-element.6) | data formatting | bytes 262144
  25.1 0.7 %copy.25 = f32[16,16,128]{2,1,0:T(8,128)} copy(f32[16,16,128]{2,1,0:T(8,128)S(1)} %get-tuple-element.7) | data formatting | bytes 262144
  25.8 0.7 %copy.26 = f32[16,16,128]{2,1,0:T(8,128)} copy(f32[16,16,128]{2,1,0:T(8,128)S(1)} %get-tuple-element.8) | data formatting | bytes 262144

commit v5 on v4

--- a/solution.py
+++ b/solution.py
@@ -12,7 +12,7 @@
 TOP = 8
 LANES = 128
 DIRS = tuple((dx, dy) for dx in (-1, 0, 1) for dy in (-1, 0, 1) if (dx, dy) != (0, 0))
-DIRS = tuple(sorted(DIRS, key=lambda d: abs(d[0]) + abs(d[1])))
+DIRS = tuple(sorted(DIRS, key=lambda d: (abs(d[0]) + abs(d[1]), abs(d[0]))))
 MESH = pl.DeviceIdType.MESH
 
 
@@ -166,13 +166,13 @@
         ).wait_recv()
         return carry
 
+    gathered[me] = window[...]
+    pl.semaphore_wait(barrier, n - 1)
     for g in range(2):
         for f in range(2):
             loads["now", g, f].wait()
-    gathered[me] = window[...]
-    pl.semaphore_wait(barrier, n - 1)
+    lax.fori_loop(1, n, far_start, 0)
     send_halo(0, 0)
-    lax.fori_loop(1, n, far_start, 0)
     send_halo(1, 0)
 
     for i in range(5):
@@ -325,6 +325,15 @@
             finish_halo(g, level)
 
 
+def write_out(*refs):
+    values, results, done = refs[:3], refs[3:6], refs[6]
+    copies = [pltpu.make_async_copy(values[i], results[i], done.at[i]) for i in range(3)]
+    for copy in copies:
+        copy.start()
+    for copy in copies:
+        copy.wait()
+
+
 def per_device(*args):
     nx, ny, nz = args[0].shape
     n_gx, n_gy = lax.axis_size("gx"), lax.axis_size("gy")
@@ -336,9 +345,10 @@
     positions = [r.reshape(n_rec // LANES, LANES) for r in (receiver_x, receiver_y)]
     anywhere = pl.BlockSpec(memory_space=pltpu.HBM)
     block = jax.ShapeDtypeStruct((nx, ny, nz), jnp.float32)
-    return pl.pallas_call(
+    held = pltpu.VMEM((nx, ny, nz), jnp.float32)
+    ends = pl.pallas_call(
         functools.partial(kernel, sizes),
-        out_shape=(block,) * 3,
+        out_shape=(held,) * 3,
         in_specs=[anywhere] * 16 + [pl.BlockSpec(memory_space=pltpu.SMEM)],
         out_specs=(pl.BlockSpec(memory_space=pltpu.VMEM),) * 3,
         scratch_shapes=[
@@ -362,6 +372,15 @@
         ),
         name="window",
     )(*[pltpu.with_memory_space_constraint(a, pltpu.HBM) for a in (*args[:13], traces, *positions)], segment_start)
+    return pl.pallas_call(
+        write_out,
+        out_shape=(block,) * 3,
+        in_specs=[pl.BlockSpec(memory_space=pltpu.VMEM)] * 3,
+        out_specs=(pl.BlockSpec(memory_space=pltpu.HBM),) * 3,
+        scratch_shapes=[pltpu.SemaphoreType.DMA((3,))],
+        compiler_params=pltpu.CompilerParams(vmem_limit_bytes=1024 * 1024),
+        name="write_out",
+    )(*[pltpu.with_memory_space_constraint(end, pltpu.VMEM) for end in ends])
 
 
 def solution(mesh):

time: 26.6 us -> 25.1 us (0.944)
  local copies, waits for them, and re-layouts: 1.97 us -> 0 us
  Pallas kernels: 23.1 us -> 23.6 us
    unnamed x3 -> x0, local copies, waits for them, and re-layouts: 1.97 us -> none
    pallas_call x1 -> x2, Pallas kernels: 23.1 us -> 23.6 us  [the longest x1 22.9 us: per_device(): pl.pallas_call(functools.partial(kernel, sizes), out_shape=(held,) * 3, i...]
where the time goes in v5:
time: 25.1 us; the launch traced here: 24.9 us
  Pallas kernels  23.6 us (94%)
  between operations  1.29 us (5%)
    pallas_call x1, Pallas kernels, per_device(): pl.pallas_call(functools.partial(kernel, sizes), out_shape=(held,) * 3, i...  22.9 us
    pallas_call x1, Pallas kernels, per_device(): pl.pallas_call(write_out, out_shape=(block,) * 3, in_specs=[pl.BlockSpec(...  0.77 us

profile of v5, /device:TPU:1, one launch (start us, length us, event | category | flops | bytes accessed | tf_op | source)
XLA Modules:
  0.0 24.9 jit_solution(11345733060331823435)
XLA Ops:
  1.3 22.9 %window.1 = (f32[16,16,128]{2,1,0:T(8,128)S(1)}, f32[16,16,128]{2,1,0:T(8,128)S(1)}, f32[16,16,128]{2,1,0:T(8,128)S(1)}) custom-call(f32[16,16,128]{2,1,0:T(8,128)} %refs_0_.1, f32[16,16,128]{2,1,0:T(8,128)} %refs_1_.1, f32[16,16,128]{2,1,0:T(8,128)} %refs_2_.1, f32[16,16,128]{2,1,0:T(8,128)} %refs_3_.1, f32[16,16,128]{2,1,0:T(8,128)} %refs_4_.1, ...), custom_call_target="tpu_custom_call" | custom-call | tf_op jit(solution)/shard_map/window/pallas_call | solution.py:349
  24.2 0.8 %write_out.1 = (f32[16,16,128]{2,1,0:T(8,128)}, f32[16,16,128]{2,1,0:T(8,128)}, f32[16,16,128]{2,1,0:T(8,128)}) custom-call(f32[16,16,128]{2,1,0:T(8,128)S(1)} %get-tuple-element.6.refs_0_, f32[16,16,128]{2,1,0:T(8,128)S(1)} %get-tuple-element.7.refs_1_, f32[16,16,128]{2,1,0:T(8,128)S(1)} %get-tuple-element.8.refs_2_), custom_call_target="tpu_custom_call" | custom-call | tf_op jit(solution)/shard_map/write_out/pallas_call | solution.py:375
